TPU v7x, 256 devices: a whole 4x4x8 slice. The times are simulated.
256 devices in a mesh: row: 32 (over y, x, core), depth: 8 (over z).
Axes of the slice: x: 4, y: 4, z: 8, core: 2. Of those that a mesh axis runs over, the one named last changes fastest.
Arguments:
- density: float32 [128, 512, 1024], P('depth', 'row'), may hold values from 0.2 to 1.5
- velocity: float32 [3, 128, 512, 1024], P(None, 'depth', 'row'), may hold values from -3 to 3
- palette: float32 [3, 4], replicated, may hold values from -6 to 6
Outputs:
- filtered: float32 [4, 512, 1024], P(None, 'row', 'depth')
- settled_density: float32 [128, 512, 1024], P('depth', 'row')
- settled_velocity: float32 [3, 128, 512, 1024], P(None, 'depth', 'row')
All inputs are finite; a program needn't handle non-finite values.
Results may differ from a plain program's by a relative error of at most 0.00013.
Values sent between devices are 32-bit elements; how exact they have to be, the bound alone decides.
A program may use at most 128 MiB of HBM per device.

v0:
```python
import math

import jax
import jax.numpy as jnp
from jax import lax
from jax.sharding import PartitionSpec as P

DIFFUSION = 0.1
ADVECTION = 0.25
VISCOSITY = 0.15
FRICTION = 0.2
OPTICAL = 2.0
RANGE_SCALE = 0.1
SPACE_SCALE = 1.5


def extended_2(block, sides, width):
    for axis, dim in sides:
        count = lax.axis_size(axis)
        forward = [(i, i + 1) for i in range(count - 1)]
        backward = [(target, source) for source, target in forward]
        low = lax.ppermute(
            lax.slice_in_dim(block, block.shape[dim] - width, None, axis=dim), axis, forward
        )
        high = lax.ppermute(lax.slice_in_dim(block, 0, width, axis=dim), axis, backward)
        block = jnp.concatenate([low, block, high], axis=dim)
    return block


def partner(array, axis, bit):
    return lax.ppermute(array, axis, [(i, i ^ 1 << bit) for i in range(lax.axis_size(axis))])


def advance(padded):
    widened = jnp.pad(padded, ((0, 0), (0, 0), (0, 0), (1, 1)))
    centre = widened[:, 1:-1, 1:-1, 1:-1]
    front_side = widened[:, :-2, 1:-1, 1:-1]
    back_side = widened[:, 2:, 1:-1, 1:-1]
    upper_side = widened[:, 1:-1, :-2, 1:-1]
    lower_side = widened[:, 1:-1, 2:, 1:-1]
    left_side = widened[:, 1:-1, 1:-1, :-2]
    right_side = widened[:, 1:-1, 1:-1, 2:]
    laplace = (
        front_side + back_side + upper_side + lower_side + left_side + right_side - 6.0 * centre
    )
    flux_div = 0.5 * (
        right_side[0] * right_side[1]
        - left_side[0] * left_side[1]
        + lower_side[0] * lower_side[2]
        - upper_side[0] * upper_side[2]
        + back_side[0] * back_side[3]
        - front_side[0] * front_side[3]
    )
    density = centre[0]
    squared = density * density
    new_density = density + DIFFUSION * laplace[0] - ADVECTION * flux_div
    viscous = VISCOSITY * squared / (1.0 + squared)
    new_velocity = (centre[1:] + viscous * laplace[1:]) / (1.0 + FRICTION * squared)
    return jnp.concatenate([new_density[None], new_velocity], 0)


def bilateral(padded, valid):
    height = padded.shape[1] - 4
    width = padded.shape[2] - 4
    luminance = (padded[0] + padded[1] + padded[2]) / 3.0
    centre_lum = luminance[2 : 2 + height, 2 : 2 + width]
    numerator = jnp.zeros((4, height, width), jnp.float32)
    denominator = jnp.zeros((height, width), jnp.float32)
    for row_offset in range(5):
        for col_offset in range(5):
            spatial = math.exp(
                -((row_offset - 2) * (row_offset - 2) + (col_offset - 2) * (col_offset - 2))
                / (2.0 * SPACE_SCALE * SPACE_SCALE)
            )
            shifted = padded[:, row_offset : row_offset + height, col_offset : col_offset + width]
            shifted_lum = luminance[
                row_offset : row_offset + height, col_offset : col_offset + width
            ]
            shifted_valid = valid[row_offset : row_offset + height, col_offset : col_offset + width]
            diff = shifted_lum - centre_lum
            weight = (
                shifted_valid * spatial * jnp.exp(-diff * diff / (2.0 * RANGE_SCALE * RANGE_SCALE))
            )
            numerator = numerator + weight[None] * shifted
            denominator = denominator + weight
    return numerator / denominator[None]


def over(front_part, back_part):
    return front_part + (1.0 - front_part[3:4]) * back_part


def body(density, velocity, palette):
    volume = jnp.concatenate([density[None], velocity], 0)
    depth_cells = volume.shape[1]
    row_cells = volume.shape[2]
    columns = volume.shape[3]
    depth_count = lax.axis_size("depth")
    row_count = lax.axis_size("row")
    depth_rank = lax.axis_index("depth")
    row_rank = lax.axis_index("row")
    for repeat_index in range(2):
        padded = extended_2(volume, (("row", 2), ("depth", 1)), 1)
        volume = advance(padded)
    settled = volume[0]
    optical = OPTICAL / (depth_cells * depth_count) * settled * settled
    opacity = 1.0 - jnp.exp(-optical)
    shading = jax.nn.sigmoid(
        jnp.einsum("ck,kzyx->czyx", palette, volume, precision=lax.Precision.HIGHEST)
    )
    before = jnp.cumsum(optical, axis=0) - optical
    weight = jnp.exp(-before) * opacity
    colour = jnp.sum(weight[None] * shading, axis=1)
    coverage = 1.0 - jnp.exp(-jnp.sum(optical, axis=0))
    picture = jnp.concatenate([colour, coverage[None]], 0)
    bit_count = depth_count.bit_length() - 1
    piece_cols = columns // depth_count
    partial_value = picture.reshape((4, row_cells) + (2,) * bit_count + (piece_cols,))
    for bit_number in range(bit_count):
        axis_pos = 2 + bit_count - bit_number - 1
        own_bit = depth_rank >> bit_number & 1
        is_front = own_bit == 0
        lower_half = lax.index_in_dim(partial_value, 0, axis_pos, False)
        upper_half = lax.index_in_dim(partial_value, 1, axis_pos, False)
        kept_half = jnp.where(is_front, lower_half, upper_half)
        outgoing = jnp.where(is_front, upper_half, lower_half)
        incoming = partner(outgoing, "depth", bit_number)
        partial_value = jnp.where(is_front, over(kept_half, incoming), over(incoming, kept_half))
    extended = extended_2(partial_value, (("row", 1), ("depth", 2)), 2)
    row_glob = row_rank * row_cells - 2 + jnp.arange(row_cells + 4, dtype=jnp.int32)
    col_glob = depth_rank * piece_cols - 2 + jnp.arange(piece_cols + 4, dtype=jnp.int32)
    row_valid = (row_glob >= 0) & (row_glob < row_cells * row_count)
    col_valid = (col_glob >= 0) & (col_glob < columns)
    valid = (row_valid[:, None] & col_valid[None, :]).astype(jnp.float32)
    filtered = bilateral(extended, valid)
    return (filtered, volume[0], volume[1:])


def solution(mesh):
    in_specs = (P("depth", "row", None), P(None, "depth", "row", None), P())
    out_specs = (P(None, "row", "depth"), P("depth", "row", None), P(None, "depth", "row", None))
    return jax.shard_map(body, mesh=mesh, in_specs=in_specs, out_specs=out_specs, check_vma=False)
```

profile of v0, /device:TPU:39, one launch (start us, length us, event | category | flops | bytes accessed | tf_op | source)
XLA Modules:
  0.0 257.6 jit_solution(5828574891187949698)
XLA Ops:
  0.7 4.2 %copy.28 = f32[3,16,16,1024]{3,0,2,1:T(4,128)S(1)} copy(f32[3,16,16,1024]{3,2,1,0:T(8,128)} %param.4) | data formatting | bytes 6291456 | tf_op args[1]
  7.1 3.7 %collective-permute-start = (f32[4,16,1,1024]{3,0,2,1:T(4,128)S(1)}, f32[4,16,1,1024]{3,0,2,1:T(4,128)S(1)}, u32[]{:S(2)}, u32[]{:S(2)}) collective-permute-start(f32[4,16,1,1024]{3,0,2,1:T(4,128)S(1)} %get-tuple-element.58), channel_id=1, source_target_pairs={{0,8},{8,16},{16,24},{24,32},{32,40},{40,48},{48,56},{56,64},{64,7... | collective-permute-start | bytes 786440 | tf_op jit(solution)/shard_map/ppermute | solution.py:22
  14.0 6.5 %collective-permute-done.1 = f32[4,16,1,1024]{3,0,2,1:T(4,128)S(1)} collective-permute-done((f32[4,16,1,1024]{3,0,2,1:T(4,128)S(1)}, f32[4,16,1,1024]{3,0,2,1:T(4,128)S(1)}, u32[]{:S(2)}, u32[]{:S(2)}) %collective-permute-start.1) | collective-permute-done | bytes 262176 | tf_op jit(solution)/shard_map/ppermute | solution.py:25
  21.8 3.5 %collective-permute-start.2 = (f32[4,1,18,1024]{3,0,2,1:T(4,128)S(1)}, f32[4,1,18,1024]{3,0,2,1:T(4,128)S(1)}, u32[]{:S(2)}, u32[]{:S(2)}) collective-permute-start(f32[4,1,18,1024]{3,0,2,1:T(4,128)S(1)} %get-tuple-element.50), channel_id=1, source_target_pairs={{0,1},{1,2},{2,3},{3,4},{4,5},{5,6},{6,7},{8,9},{9,10},{10,11},{11... | collective-permute-start | bytes 884744 | tf_op jit(solution)/shard_map/ppermute | solution.py:22
  25.4 2.4 collective-permute-start.3
  27.9 6.2 %maximum_maximum_fusion.2 = (f32[4,16,17,1024]{3,0,2,1:T(4,128)}, f32[4,16,17,1024]{3,0,2,1:T(4,128)}) fusion(f32[3,16,16,1024]{3,0,2,1:T(4,128)S(1)} %copy-done.2, f32[1,16,16,1024]{3,0,2,1:T(1,128)S(1)} %broadcast_in_dim.2, f32[4,16,1,1024]{3,0,2,1:T(4,128)S(1)} %collective-permute-done, f32[4,16,1,1024]{3,0,2,1:T(4,128)S(1)} %collective-permute-done.1), kind=kLoop, calls=%fused_computation.23 | loop fusion | flops 4456448 | bytes 13631488 | tf_op jit(solution)/shard_map/concatenate | solution.py:26
  34.0 6.5 %maximum_maximum_fusion = (f32[4,17,18,1024]{3,0,2,1:T(4,128)}, f32[4,17,18,1024]{3,0,2,1:T(4,128)}) fusion(f32[4,16,1,1024]{3,0,2,1:T(4,128)S(1)} %collective-permute-done.1, f32[3,16,16,1024]{3,0,2,1:T(4,128)S(1)} %copy-done.2, f32[1,16,16,1024]{3,0,2,1:T(1,128)S(1)} %broadcast_in_dim.2, f32[4,16,1,1024]{3,0,2,1:T(4,128)S(1)} %collective-permute-done, ...), kind=kLoop, calls=%fused_computation.19 | loop fusion | flops 10027008 | bytes 15335424 | tf_op jit(solution)/shard_map/concatenate | solution.py:26
  40.6 15.4 %select_maximum_fusion.5 = f32[4,18,18,1026]{3,0,2,1:T(4,128)S(1)} fusion(f32[4,1,18,1024]{3,0,2,1:T(4,128)S(1)} %collective-permute-done.3, f32[4,1,18,1024]{3,0,2,1:T(4,128)S(1)} %collective-permute-done.2, f32[4,16,1,1024]{3,0,2,1:T(4,128)S(1)} %collective-permute-done.1, f32[4,16,1,1024]{3,0,2,1:T(4,128)S(1)} %collective-permute-done, ...), kind=kLoop, calls=%fused_computation.13 | loop fusion | flops 18615744 | bytes 10627200 | tf_op jit(solution)/shard_map/concatenate | solution.py:26
  55.9 10.4 %fusion.4 = f32[4,16,16,1024]{3,0,2,1:T(4,128)} fusion(f32[1,16,16,1024]{3,0,2,1:T(1,128)S(1)} %broadcast_in_dim.2, f32[4,18,18,1026]{3,0,2,1:T(4,128)S(1)} %select_maximum_fusion.5, f32[4,16,17,1024]{3,0,2,1:T(4,128)} %get-tuple-element.57, f32[4,16,17,1024]{3,0,2,1:T(4,128)} %get-tuple-element.56, f32[4,17,18,1024]{3,0,2,1:T(4,128)} %get-tuple-element.49, ...), kind=kLoop, calls=%fused_computation.30 | loop fusion | flops 8388608 | bytes 33554432 | tf_op jit(solution)/shard_map/sub | solution.py:44
  66.4 32.9 %add_divide_fusion = (f32[1,16,16,1024]{3,0,2,1:T(1,128)S(1)}, f32[1,16,16,1024]{3,0,2,1:T(1,128)S(1)}) fusion(f32[4,16,1,1024]{3,0,2,1:T(4,128)S(1)} %collective-permute-done.1, f32[3,16,16,1024]{3,0,2,1:T(4,128)S(1)} %copy-done.2, f32[1,16,16,1024]{3,0,2,1:T(1,128)S(1)} %broadcast_in_dim.2, f32[4,16,1,1024]{3,0,2,1:T(4,128)S(1)} %collective-permute-done, ...), kind=kLoop, calls=%fused_computation.96 | loop fusion | flops 11272192 | bytes 12648448 | tf_op jit(solution)/shard_map/div | solution.py:57
  100.8 4.2 %fusion.8 = f32[3,16,16,1024]{3,0,2,1:T(4,128)S(1)} fusion(f32[4,16,16,1024]{3,0,2,1:T(4,128)S(1)} %copy-done.3, f32[16,16,1024]{2,1,0:T(8,128)S(1)} %get-tuple-element.61, f32[16,16,1024]{2,1,0:T(8,128)S(1)} %get-tuple-element.60, f32[3,16,16,1024]{3,2,1,0:T(8,128)S(1)} %copy-done.5), kind=kLoop, calls=%fused_computation.41 | loop fusion | flops 2359296 | bytes 11534336 | tf_op jit(solution)/shard_map/div | solution.py:58
  105.3 3.7 %collective-permute-start.4 = (f32[4,16,1,1024]{3,0,2,1:T(4,128)S(1)}, f32[4,16,1,1024]{3,0,2,1:T(4,128)S(1)}, u32[]{:S(2)}, u32[]{:S(2)}) collective-permute-start(f32[4,16,1,1024]{3,0,2,1:T(4,128)S(1)} %get-tuple-element.54), channel_id=1, source_target_pairs={{0,8},{8,16},{16,24},{24,32},{32,40},{40,48},{48,56},{56,64},{64,7... | collective-permute-start | bytes 786440 | tf_op jit(solution)/shard_map/ppermute | solution.py:22
  109.0 1.9 collective-permute-start.5
  112.4 6.4 %collective-permute-done.5 = f32[4,16,1,1024]{3,0,2,1:T(4,128)S(1)} collective-permute-done((f32[4,16,1,1024]{3,0,2,1:T(4,128)S(1)}, f32[4,16,1,1024]{3,0,2,1:T(4,128)S(1)}, u32[]{:S(2)}, u32[]{:S(2)}) %collective-permute-start.5) | collective-permute-done | bytes 262176 | tf_op jit(solution)/shard_map/ppermute | solution.py:25
  119.1 4.8 %collective-permute-start.6 = (f32[4,1,18,1024]{3,0,2,1:T(4,128)S(1)}, f32[4,1,18,1024]{3,0,2,1:T(4,128)S(1)}, u32[]{:S(2)}, u32[]{:S(2)}) collective-permute-start(f32[4,1,18,1024]{3,0,2,1:T(4,128)S(1)} %get-tuple-element.46), channel_id=1, source_target_pairs={{0,1},{1,2},{2,3},{3,4},{4,5},{5,6},{6,7},{8,9},{9,10},{10,11},{11... | collective-permute-start | bytes 884744 | tf_op jit(solution)/shard_map/ppermute | solution.py:22
  125.8 6.1 %maximum_maximum_fusion.3 = (f32[4,16,17,1024]{3,0,2,1:T(4,128)}, f32[4,16,17,1024]{3,0,2,1:T(4,128)}) fusion(f32[3,16,16,1024]{3,0,2,1:T(4,128)S(1)} %fusion.8, f32[1,16,16,1024]{3,0,2,1:T(1,128)S(1)} %get-tuple-element.43, f32[4,16,1,1024]{3,0,2,1:T(4,128)S(1)} %collective-permute-done.4, f32[4,16,1,1024]{3,0,2,1:T(4,128)S(1)} %collective-permute-done.5), kind=kLoop, calls=%fused_computation.25 | loop fusion | flops 4456448 | bytes 13631488 | tf_op jit(solution)/shard_map/concatenate | solution.py:26
  132.5 6.5 %maximum_maximum_fusion.1 = (f32[4,17,18,1024]{3,0,2,1:T(4,128)}, f32[4,17,18,1024]{3,0,2,1:T(4,128)}) fusion(f32[4,16,1,1024]{3,0,2,1:T(4,128)S(1)} %collective-permute-done.5, f32[3,16,16,1024]{3,0,2,1:T(4,128)S(1)} %fusion.8, f32[1,16,16,1024]{3,0,2,1:T(1,128)S(1)} %get-tuple-element.43, f32[4,16,1,1024]{3,0,2,1:T(4,128)S(1)} %collective-permute-done.4, ...), kind=kLoop, calls=%fused_computation.21 | loop fusion | flops 10027008 | bytes 15335424 | tf_op jit(solution)/shard_map/concatenate | solution.py:26
  139.0 15.4 %select_maximum_fusion = f32[4,18,18,1026]{3,0,2,1:T(4,128)S(1)} fusion(f32[4,1,18,1024]{3,0,2,1:T(4,128)S(1)} %collective-permute-done.7, f32[4,1,18,1024]{3,0,2,1:T(4,128)S(1)} %collective-permute-done.6, f32[4,16,1,1024]{3,0,2,1:T(4,128)S(1)} %collective-permute-done.5, f32[4,16,1,1024]{3,0,2,1:T(4,128)S(1)} %collective-permute-done.4, ...), kind=kLoop, calls=%fused_computation.8 | loop fusion | flops 18615744 | bytes 10627200 | tf_op jit(solution)/shard_map/concatenate | solution.py:26
  154.5 9.1 %fusion.2 = f32[4,16,16,1024]{3,0,2,1:T(4,128)S(1)} fusion(f32[1,16,16,1024]{3,0,2,1:T(1,128)S(1)} %get-tuple-element.43, f32[4,18,18,1026]{3,0,2,1:T(4,128)S(1)} %select_maximum_fusion, f32[4,16,17,1024]{3,0,2,1:T(4,128)} %get-tuple-element.53, f32[4,16,17,1024]{3,0,2,1:T(4,128)} %get-tuple-element.52, f32[4,17,18,1024]{3,0,2,1:T(4,128)} %get-tuple-element.45, ...), kind=kLoop, calls=%fused_computation.28 | loop fusion | flops 8388608 | bytes 33554432 | tf_op jit(solution)/shard_map/sub | solution.py:44
  163.6 32.1 %multiply_multiply_fusion.1 = (f32[1,16,16,1024]{3,0,2,1:T(1,128)S(1)}, f32[1,16,16,1024]{3,0,2,1:T(1,128)S(1)}) fusion(f32[4,16,1,1024]{3,0,2,1:T(4,128)S(1)} %collective-permute-done.5, f32[3,16,16,1024]{3,0,2,1:T(4,128)S(1)} %fusion.8, f32[1,16,16,1024]{3,0,2,1:T(1,128)S(1)} %get-tuple-element.43, f32[4,16,1,1024]{3,0,2,1:T(4,128)S(1)} %collective-permute-done.4, ...), kind=kLoop, calls=%fused_computation.57 | loop fusion | flops 10747904 | bytes 12648448 | tf_op jit(solution)/shard_map/mul | solution.py:106
  197.3 2.7 %subtract_multiply_fusion = f32[1,16,16,1024]{3,0,2,1:T(1,128)S(1)} fusion(f32[1,16,16,1024]{3,2,1,0:T(8,128)S(1)} %fusion.31, f32[1,16,16,1024]{3,0,2,1:T(1,128)S(1)} %get-tuple-element.41), kind=kLoop, calls=%fused_computation.97 | loop fusion | flops 1835008 | bytes 3145728 | tf_op jit(solution)/shard_map/mul | solution.py:112
  200.2 2.8 %fusion.6 = f32[3,16,16,1024]{3,0,2,1:T(4,128)S(1)} fusion(f32[3,16,16,1024]{3,0,2,1:T(4,128)S(1)} %fusion.8, f32[4,16,16,1024]{3,0,2,1:T(4,128)S(1)} %fusion.2, f32[16,16,1024]{2,1,0:T(8,128)S(1)} %get-tuple-element.77, f32[16,16,1024]{2,1,0:T(8,128)S(1)} %copy-done.6), kind=kLoop, calls=%fused_computation.33 | loop fusion | flops 2359296 | bytes 11534336 | tf_op jit(solution)/shard_map/div | solution.py:58
  203.0 10.9 %multiply_reduce_fusion = f32[16,1024,3]{1,2,0:T(4,128)S(1)} fusion(f32[3,16,16,1024]{3,0,2,1:T(4,128)S(1)} %fusion.6, f32[1,16,16,1024]{3,0,2,1:T(1,128)S(1)} %get-tuple-element.41, f32[16,16,1024]{2,1,0:T(8,128)S(1)} %bitcast.77, f32[3,4]{1,0:T(4,128)S(1)} %copy-done), kind=kOutput, calls=%fused_computation.51 | convolution fusion | flops 42680320 | bytes 5439536 | tf_op jit(solution)/shard_map/ck,kzyx->czyx/dot_general | solution.py:109
  214.7 3.7 %collective-permute-done.8 = f32[4,16,2,2,128]{4,3,2,1,0:T(2,128)S(1)} collective-permute-done((f32[4,16,2,2,128]{4,3,2,1,0:T(2,128)S(1)}, f32[4,16,2,2,128]{4,3,2,1,0:T(2,128)S(1)}, u32[]{:S(2)}, u32[]{:S(2)}) %collective-permute-start.8) | collective-permute-done | bytes 131104 | tf_op jit(solution)/shard_map/ppermute | solution.py:31
  218.6 3.3 %collective-permute-start.9 = (f32[4,16,2,128]{3,2,1,0:T(2,128)S(1)}, f32[4,16,2,128]{3,2,1,0:T(2,128)S(1)}, u32[]{:S(2)}, u32[]{:S(2)}) collective-permute-start(f32[4,16,2,128]{3,2,1,0:T(2,128)S(1)} %bitcast.88), channel_id=1, source_target_pairs={{0,2},{1,3},{2,0},{3,1},{4,6},{5,7},{6,4},{7,5},{8,10},{9,11},{10,... | collective-permute-start | bytes 196616 | tf_op jit(solution)/shard_map/ppermute | solution.py:31
  223.8 3.4 %collective-permute-start.10 = (f32[4,16,128]{2,1,0:T(8,128)S(1)}, f32[4,16,128]{2,1,0:T(8,128)S(1)}, u32[]{:S(2)}, u32[]{:S(2)}) collective-permute-start(f32[4,16,128]{2,1,0:T(8,128)S(1)} %bitcast.89), channel_id=1, source_target_pairs={{0,4},{1,5},{2,6},{3,7},{4,0},{5,1},{6,2},{7,3},{8,12},{9,13},{10,... | collective-permute-start | bytes 98312 | tf_op jit(solution)/shard_map/ppermute | solution.py:31
  227.1 3.4 %collective-permute-done.10 = f32[4,16,128]{2,1,0:T(8,128)S(1)} collective-permute-done((f32[4,16,128]{2,1,0:T(8,128)S(1)}, f32[4,16,128]{2,1,0:T(8,128)S(1)}, u32[]{:S(2)}, u32[]{:S(2)}) %collective-permute-start.10) | collective-permute-done | bytes 32800 | tf_op jit(solution)/shard_map/ppermute | solution.py:31
  230.5 6.8 %collective-permute-start.11 = (f32[4,2,128]{2,1,0:T(2,128)S(1)}, f32[4,2,128]{2,1,0:T(2,128)S(1)}, u32[]{:S(2)}, u32[]{:S(2)}) collective-permute-start(f32[4,2,128]{2,1,0:T(2,128)S(1)} %get-tuple-element.75), channel_id=1, source_target_pairs={{0,8},{8,16},{16,24},{24,32},{32,40},{40,48},{48,56},{56,64},{64,7... | collective-permute-start | bytes 12296 | tf_op jit(solution)/shard_map/ppermute | solution.py:22
  239.3 5.1 %collective-permute-done.12 = f32[4,2,128]{2,1,0:T(2,128)S(1)} collective-permute-done((f32[4,2,128]{2,1,0:T(2,128)S(1)}, f32[4,2,128]{2,1,0:T(2,128)S(1)}, u32[]{:S(2)}, u32[]{:S(2)}) %collective-permute-start.12) | collective-permute-done | bytes 4128 | tf_op jit(solution)/shard_map/ppermute | solution.py:25
  244.5 3.6 %collective-permute-start.13 = (f32[4,20,2]{2,1,0:T(8,128)S(1)}, f32[4,20,2]{2,1,0:T(8,128)S(1)}, u32[]{:S(2)}, u32[]{:S(2)}) collective-permute-start(f32[4,20,2]{2,1,0:T(8,128)S(1)} %get-tuple-element.71), channel_id=1, source_target_pairs={{0,1},{1,2},{2,3},{3,4},{4,5},{5,6},{6,7},{8,9},{9,10},{10,11},{11... | collective-permute-start | bytes 1928 | tf_op jit(solution)/shard_map/ppermute | solution.py:22
  248.1 2.2 collective-permute-start.14
  250.4 5.7 %copy.45 = f32[3,16,16,1024]{3,2,1,0:T(8,128)} copy(f32[3,16,16,1024]{3,0,2,1:T(4,128)} %copy-done.4) | data formatting | bytes 6291456
  (71 shorter events, 20.6 us)
Async XLA Ops:
  0.6 202.3 %copy-start = (f32[3,4]{1,0:T(4,128)S(1)}, f32[3,4]{1,0:T(4,128)}, u32[]{:S(2)}) copy-start(f32[3,4]{1,0:T(4,128)} %param.5) | copy-start | bytes 148
  0.6 4.2 %copy-start.7 = (f32[16,16,1024]{2,1,0:T(8,128)S(1)}, f32[16,16,1024]{2,1,0:T(8,128)}, u32[]{:S(2)}) copy-start(f32[16,16,1024]{2,1,0:T(8,128)} %param.3) | copy-start | bytes 3145732
  4.9 2.0 copy-start.1
  7.1 7.0 %collective-permute-start = (f32[4,16,1,1024]{3,0,2,1:T(4,128)S(1)}, f32[4,16,1,1024]{3,0,2,1:T(4,128)S(1)}, u32[]{:S(2)}, u32[]{:S(2)}) collective-permute-start(f32[4,16,1,1024]{3,0,2,1:T(4,128)S(1)} %get-tuple-element.58), channel_id=1, source_target_pairs={{0,8},{8,16},{16,24},{24,32},{32,40},{40,48},{48,56},{56,64},{64,7... | collective-permute-start | bytes 786440 | tf_op jit(solution)/shard_map/ppermute | solution.py:22
  10.7 9.8 %collective-permute-start.1 = (f32[4,16,1,1024]{3,0,2,1:T(4,128)S(1)}, f32[4,16,1,1024]{3,0,2,1:T(4,128)S(1)}, u32[]{:S(2)}, u32[]{:S(2)}) collective-permute-start(f32[4,16,1,1024]{3,0,2,1:T(4,128)S(1)} %get-tuple-element.59), channel_id=1, source_target_pairs={{8,0},{16,8},{24,16},{32,24},{40,32},{48,40},{56,48},{64,56},{72,6... | collective-permute-start | bytes 786440 | tf_op jit(solution)/shard_map/ppermute | solution.py:25
  12.7 15.1 %copy-start.2 = (f32[3,16,16,1024]{3,0,2,1:T(4,128)S(1)}, f32[3,16,16,1024]{3,0,2,1:T(4,128)}, u32[]{:S(2)}) copy-start(f32[3,16,16,1024]{3,0,2,1:T(4,128)} %copy-done.1) | copy-start | bytes 9437188
  21.8 12.2 %collective-permute-start.2 = (f32[4,1,18,1024]{3,0,2,1:T(4,128)S(1)}, f32[4,1,18,1024]{3,0,2,1:T(4,128)S(1)}, u32[]{:S(2)}, u32[]{:S(2)}) collective-permute-start(f32[4,1,18,1024]{3,0,2,1:T(4,128)S(1)} %get-tuple-element.50), channel_id=1, source_target_pairs={{0,1},{1,2},{2,3},{3,4},{4,5},{5,6},{6,7},{8,9},{9,10},{10,11},{11... | collective-permute-start | bytes 884744 | tf_op jit(solution)/shard_map/ppermute | solution.py:22
  25.4 8.6 %collective-permute-start.3 = (f32[4,1,18,1024]{3,0,2,1:T(4,128)S(1)}, f32[4,1,18,1024]{3,0,2,1:T(4,128)S(1)}, u32[]{:S(2)}, u32[]{:S(2)}) collective-permute-start(f32[4,1,18,1024]{3,0,2,1:T(4,128)S(1)} %get-tuple-element.51), channel_id=1, source_target_pairs={{1,0},{2,1},{3,2},{4,3},{5,4},{6,5},{7,6},{9,8},{10,9},{11,10},{12... | collective-permute-start | bytes 884744 | tf_op jit(solution)/shard_map/ppermute | solution.py:25
  66.4 34.4 %copy-start.3 = (f32[4,16,16,1024]{3,0,2,1:T(4,128)S(1)}, f32[4,16,16,1024]{3,0,2,1:T(4,128)}, u32[]{:S(2)}) copy-start(f32[4,16,16,1024]{3,0,2,1:T(4,128)} %fusion.4) | copy-start | bytes 12582916
  66.4 34.4 %copy-start.5 = (f32[3,16,16,1024]{3,2,1,0:T(8,128)S(1)}, f32[3,16,16,1024]{3,2,1,0:T(8,128)}, u32[]{:S(2)}) copy-start(f32[3,16,16,1024]{3,2,1,0:T(8,128)} %param.4) | copy-start | bytes 9437188
  105.3 7.1 %collective-permute-start.4 = (f32[4,16,1,1024]{3,0,2,1:T(4,128)S(1)}, f32[4,16,1,1024]{3,0,2,1:T(4,128)S(1)}, u32[]{:S(2)}, u32[]{:S(2)}) collective-permute-start(f32[4,16,1,1024]{3,0,2,1:T(4,128)S(1)} %get-tuple-element.54), channel_id=1, source_target_pairs={{0,8},{8,16},{16,24},{24,32},{32,40},{40,48},{48,56},{56,64},{64,7... | collective-permute-start | bytes 786440 | tf_op jit(solution)/shard_map/ppermute | solution.py:22
  109.0 9.8 %collective-permute-start.5 = (f32[4,16,1,1024]{3,0,2,1:T(4,128)S(1)}, f32[4,16,1,1024]{3,0,2,1:T(4,128)S(1)}, u32[]{:S(2)}, u32[]{:S(2)}) collective-permute-start(f32[4,16,1,1024]{3,0,2,1:T(4,128)S(1)} %get-tuple-element.55), channel_id=1, source_target_pairs={{8,0},{16,8},{24,16},{32,24},{40,32},{48,40},{56,48},{64,56},{72,6... | collective-permute-start | bytes 786440 | tf_op jit(solution)/shard_map/ppermute | solution.py:25
  119.1 12.8 %collective-permute-start.6 = (f32[4,1,18,1024]{3,0,2,1:T(4,128)S(1)}, f32[4,1,18,1024]{3,0,2,1:T(4,128)S(1)}, u32[]{:S(2)}, u32[]{:S(2)}) collective-permute-start(f32[4,1,18,1024]{3,0,2,1:T(4,128)S(1)} %get-tuple-element.46), channel_id=1, source_target_pairs={{0,1},{1,2},{2,3},{3,4},{4,5},{5,6},{6,7},{8,9},{9,10},{10,11},{11... | collective-permute-start | bytes 884744 | tf_op jit(solution)/shard_map/ppermute | solution.py:22
  123.8 8.7 %collective-permute-start.7 = (f32[4,1,18,1024]{3,0,2,1:T(4,128)S(1)}, f32[4,1,18,1024]{3,0,2,1:T(4,128)S(1)}, u32[]{:S(2)}, u32[]{:S(2)}) collective-permute-start(f32[4,1,18,1024]{3,0,2,1:T(4,128)S(1)} %get-tuple-element.47), channel_id=1, source_target_pairs={{1,0},{2,1},{3,2},{4,3},{5,4},{6,5},{7,6},{9,8},{10,9},{11,10},{12... | collective-permute-start | bytes 884744 | tf_op jit(solution)/shard_map/ppermute | solution.py:25
  195.6 4.5 %copy-start.6 = (f32[16,16,1024]{2,1,0:T(8,128)S(1)}, f32[16,16,1024]{2,1,0:T(8,128)}, u32[]{:S(2)}) copy-start(f32[16,16,1024]{2,1,0:T(8,128)} %get-tuple-element.78) | copy-start | bytes 3145732
  202.9 10.9 %copy-start.4 = (f32[3,16,16,1024]{3,0,2,1:T(4,128)}, f32[3,16,16,1024]{3,0,2,1:T(4,128)S(1)}, u32[]{:S(2)}) copy-start(f32[3,16,16,1024]{3,0,2,1:T(4,128)S(1)} %fusion.6) | copy-start | bytes 9437188
  214.5 3.9 %collective-permute-start.8 = (f32[4,16,2,2,128]{4,3,2,1,0:T(2,128)S(1)}, f32[4,16,2,2,128]{4,3,2,1,0:T(2,128)S(1)}, u32[]{:S(2)}, u32[]{:S(2)}) collective-permute-start(f32[4,16,2,2,128]{4,3,2,1,0:T(2,128)S(1)} %bitcast.87), channel_id=1, source_target_pairs={{0,1},{1,0},{2,3},{3,2},{4,5},{5,4},{6,7},{7,6},{8,9},{9,8},{10,11... | collective-permute-start | bytes 393224 | tf_op jit(solution)/shard_map/ppermute | solution.py:31
  218.6 5.0 %collective-permute-start.9 = (f32[4,16,2,128]{3,2,1,0:T(2,128)S(1)}, f32[4,16,2,128]{3,2,1,0:T(2,128)S(1)}, u32[]{:S(2)}, u32[]{:S(2)}) collective-permute-start(f32[4,16,2,128]{3,2,1,0:T(2,128)S(1)} %bitcast.88), channel_id=1, source_target_pairs={{0,2},{1,3},{2,0},{3,1},{4,6},{5,7},{6,4},{7,5},{8,10},{9,11},{10,... | collective-permute-start | bytes 196616 | tf_op jit(solution)/shard_map/ppermute | solution.py:31
  223.8 6.8 %collective-permute-start.10 = (f32[4,16,128]{2,1,0:T(8,128)S(1)}, f32[4,16,128]{2,1,0:T(8,128)S(1)}, u32[]{:S(2)}, u32[]{:S(2)}) collective-permute-start(f32[4,16,128]{2,1,0:T(8,128)S(1)} %bitcast.89), channel_id=1, source_target_pairs={{0,4},{1,5},{2,6},{3,7},{4,0},{5,1},{6,2},{7,3},{8,12},{9,13},{10,... | collective-permute-start | bytes 98312 | tf_op jit(solution)/shard_map/ppermute | solution.py:31
  230.5 8.8 %collective-permute-start.11 = (f32[4,2,128]{2,1,0:T(2,128)S(1)}, f32[4,2,128]{2,1,0:T(2,128)S(1)}, u32[]{:S(2)}, u32[]{:S(2)}) collective-permute-start(f32[4,2,128]{2,1,0:T(2,128)S(1)} %get-tuple-element.75), channel_id=1, source_target_pairs={{0,8},{8,16},{16,24},{24,32},{32,40},{40,48},{48,56},{56,64},{64,7... | collective-permute-start | bytes 12296 | tf_op jit(solution)/shard_map/ppermute | solution.py:22
  237.4 7.0 %collective-permute-start.12 = (f32[4,2,128]{2,1,0:T(2,128)S(1)}, f32[4,2,128]{2,1,0:T(2,128)S(1)}, u32[]{:S(2)}, u32[]{:S(2)}) collective-permute-start(f32[4,2,128]{2,1,0:T(2,128)S(1)} %get-tuple-element.76), channel_id=1, source_target_pairs={{8,0},{16,8},{24,16},{32,24},{40,32},{48,40},{56,48},{64,56},{72,6... | collective-permute-start | bytes 12296 | tf_op jit(solution)/shard_map/ppermute | solution.py:25
  244.5 11.6 %collective-permute-start.13 = (f32[4,20,2]{2,1,0:T(8,128)S(1)}, f32[4,20,2]{2,1,0:T(8,128)S(1)}, u32[]{:S(2)}, u32[]{:S(2)}) collective-permute-start(f32[4,20,2]{2,1,0:T(8,128)S(1)} %get-tuple-element.71), channel_id=1, source_target_pairs={{0,1},{1,2},{2,3},{3,4},{4,5},{5,6},{6,7},{8,9},{9,10},{10,11},{11... | collective-permute-start | bytes 1928 | tf_op jit(solution)/shard_map/ppermute | solution.py:22
  248.1 7.9 %collective-permute-start.14 = (f32[4,20,2]{2,1,0:T(8,128)S(1)}, f32[4,20,2]{2,1,0:T(8,128)S(1)}, u32[]{:S(2)}, u32[]{:S(2)}) collective-permute-start(f32[4,20,2]{2,1,0:T(8,128)S(1)} %get-tuple-element.72), channel_id=1, source_target_pairs={{1,0},{2,1},{3,2},{4,3},{5,4},{6,5},{7,6},{9,8},{10,9},{11,10},{12... | collective-permute-start | bytes 1928 | tf_op jit(solution)/shard_map/ppermute | solution.py:25
where the time goes:
time: 262 us; the launch traced here: 258 us
  other arithmetic  158 us (60%)
  starting transfers between devices  45.2 us (17%)
  waiting for transfers between devices  28.4 us (11%)
  local copies, waits for them, and re-layouts  13.9 us (5%)
  matrix products  10.9 us (4%)
    concatenate x8, other arithmetic, extended_2(): block = jnp.concatenate([low, block, high], axis=dim)  56.2 us
    div x2, other arithmetic, advance(): viscous = VISCOSITY * squared / (1.0 + squared)  33.2 us
    mul x1, other arithmetic, body(): optical = OPTICAL / (depth_cells * depth_count) * settled * settled  32.1 us
    ppermute x6, starting transfers between devices, extended_2(): lax.ppermute(lax.slice_in_dim(block, block.shape[dim] - width, None, axis...  26.2 us
    sub x2, other arithmetic, advance(): front_side + back_side + upper_side + lower_side + left_side + right_side  19.5 us
    ppermute x6, waiting for transfers between devices, extended_2(): lax.ppermute(lax.slice_in_dim(block, 0, width, axis=dim), axis, backward)  18.6 us
    unnamed x21, local copies, waits for them, and re-layouts  12.7 us
    ppermute x6, starting transfers between devices, extended_2(): lax.ppermute(lax.slice_in_dim(block, 0, width, axis=dim), axis, backward)  12.3 us
  transfers between devices with their start and end apart: 15, of which 8 were waited for; matrix products, arithmetic and copies ran while one was open for 8% of the time, Pallas kernels for 0%

commit v1 on v0

v1 whole, which is shorter than its diff:
```python
import functools
import math

import jax
import jax.numpy as jnp
from jax import lax
from jax.experimental import pallas as pl
from jax.experimental.pallas import tpu as pltpu
from jax.sharding import PartitionSpec as P

DIFFUSION = 0.1
ADVECTION = 0.25
VISCOSITY = 0.15
FRICTION = 0.2
OPTICAL = 2.0
RANGE_SCALE = 0.1
SPACE_SCALE = 1.5
MESH = pl.DeviceIdType.MESH
LANES = 128
SUB = 8


def shifted_pair(before, here, after, first, last):
    left = pltpu.roll(jnp.where(last, before, here), 1, 1)
    right = pltpu.roll(jnp.where(first, after, here), LANES - 1, 1)
    return left, right


def step_tile(ref, z, block, row, first, last):
    def get(k, dz=0, dy=0, dx=0):
        return ref[k, z + dz, block + dx, pl.ds(row + dy, SUB), :]

    here = [get(k) for k in range(4)]
    sides = [
        shifted_pair(get(k, dx=-1), here[k], get(k, dx=1), first, last) for k in range(4)
    ]
    up = [get(k, dy=-1) for k in range(4)]
    down = [get(k, dy=1) for k in range(4)]
    front = [get(k, dz=-1) for k in range(4)]
    back = [get(k, dz=1) for k in range(4)]
    left = [s[0] for s in sides]
    right = [s[1] for s in sides]
    sums = [
        (left[k] + right[k]) + (up[k] + down[k]) + (front[k] + back[k]) for k in range(4)
    ]
    flux = (
        (right[0] * right[1] - left[0] * left[1])
        + (down[0] * down[2] - up[0] * up[2])
        + (back[0] * back[3] - front[0] * front[3])
    )
    r = here[0]
    squared = r * r
    new_r = (1.0 - 6.0 * DIFFUSION) * r + DIFFUSION * sums[0] - (0.5 * ADVECTION) * flux
    one = 1.0 + squared
    drag = 1.0 + FRICTION * squared
    inverse = 1.0 / (one * drag)
    side_w = VISCOSITY * squared * inverse
    own_w = one * inverse - 6.0 * side_w
    return [new_r] + [own_w * here[k] + side_w * sums[k] for k in range(1, 4)]


def kernel(
    depth_count,
    row_count,
    dens,
    vel,
    pal,
    filtered,
    out_d,
    out_v,
    q0,
    q1,
    corner_d,
    corner_v,
    piece,
    pieces,
    ext,
    load_sem,
    zsend,
    zrecv,
    rsend,
    rrecv,
    csend,
    crecv,
    psend,
    precv,
    hsend,
    hrecv,
):
    zn, yn = dens.shape[0], dens.shape[1]
    chunks = dens.shape[2] // LANES
    tiles = yn // SUB
    d = lax.axis_index("depth")
    r = lax.axis_index("row")
    has = {-1: (d > 0, r > 0), 1: (d < depth_count - 1, r < row_count - 1)}

    def present(dd, dr):
        ok = None
        for step, which in ((dd, 0), (dr, 1)):
            if step:
                ok = has[step][which] if ok is None else ok & has[step][which]
        return ok

    def where_is(dd, dr):
        return {"depth": d + dd, "row": r + dr}

    around = [(dd, dr) for dd in (-1, 0, 1) for dr in (-1, 0, 1) if dd or dr]
    diagonal = [(dd, dr) for dd in (-1, 1) for dr in (-1, 1)]

    barrier = pltpu.get_barrier_semaphore()
    count = jnp.int32(depth_count - 1)
    for dd, dr in around:
        if dr == 0:
            continue
        ok = present(dd, dr)
        count = count + ok.astype(jnp.int32)

        @pl.when(ok)
        def _(dd=dd, dr=dr):
            pl.semaphore_signal(barrier, inc=1, device_id=where_is(dd, dr), device_id_type=MESH)

    for k in range(1, depth_count):
        other = lax.rem(d + k, depth_count)
        pl.semaphore_signal(
            barrier, inc=1, device_id={"depth": other, "row": r}, device_id_type=MESH
        )

    def cols(c):
        return pl.ds(pl.multiple_of(c * LANES, LANES), LANES)

    def loads(c):
        rows = pl.ds(SUB, yn)
        return (
            pltpu.make_async_copy(
                dens.at[:, :, cols(c)], q0.at[0, pl.ds(2, zn), 1 + c, rows, :], load_sem.at[0, c]
            ),
            pltpu.make_async_copy(
                vel.at[:, :, :, cols(c)],
                q0.at[pl.ds(1, 3), pl.ds(2, zn), 1 + c, rows, :],
                load_sem.at[1, c],
            ),
        )

    def zcopies(c, dd):
        src = pl.ds(0, 2) if dd < 0 else pl.ds(zn - 2, 2)
        dst = pl.ds(zn + 2, 2) if dd < 0 else pl.ds(0, 2)
        side = (dd + 1) // 2
        rows = pl.ds(SUB, yn)
        return (
            pltpu.make_async_remote_copy(
                dens.at[src, :, cols(c)],
                q0.at[0, dst, 1 + c, rows, :],
                zsend.at[side, 0, c],
                zrecv.at[side, 0, c],
                device_id=where_is(dd, 0),
                device_id_type=MESH,
            ),
            pltpu.make_async_remote_copy(
                vel.at[:, src, :, cols(c)],
                q0.at[pl.ds(1, 3), dst, 1 + c, rows, :],
                zsend.at[side, 1, c],
                zrecv.at[side, 1, c],
                device_id=where_is(dd, 0),
                device_id_type=MESH,
            ),
        )

    def rcopies(c, dr):
        src = pl.ds(0, 2) if dr < 0 else pl.ds(yn - 2, 2)
        dst = pl.ds(SUB + yn, 2) if dr < 0 else pl.ds(SUB - 2, 2)
        side = (dr + 1) // 2
        return (
            pltpu.make_async_remote_copy(
                dens.at[:, src, cols(c)],
                q0.at[0, pl.ds(2, zn), 1 + c, dst, :],
                rsend.at[side, 0, c],
                rrecv.at[side, 0, c],
                device_id=where_is(0, dr),
                device_id_type=MESH,
            ),
            pltpu.make_async_remote_copy(
                vel.at[:, :, src, cols(c)],
                q0.at[pl.ds(1, 3), pl.ds(2, zn), 1 + c, dst, :],
                rsend.at[side, 1, c],
                rrecv.at[side, 1, c],
                device_id=where_is(0, dr),
                device_id_type=MESH,
            ),
        )

    def ccopies(dd, dr):
        z = pl.ds(0, 1) if dd < 0 else pl.ds(zn - 1, 1)
        y = pl.ds(0, 1) if dr < 0 else pl.ds(yn - 1, 1)
        slot = diagonal.index((-dd, -dr))
        return (
            pltpu.make_async_remote_copy(
                dens.at[z, y, :],
                corner_d.at[slot],
                csend.at[0, slot],
                crecv.at[0, slot],
                device_id=where_is(dd, dr),
                device_id_type=MESH,
            ),
            pltpu.make_async_remote_copy(
                vel.at[:, z, y, :],
                corner_v.at[slot],
                csend.at[1, slot],
                crecv.at[1, slot],
                device_id=where_is(dd, dr),
                device_id_type=MESH,
            ),
        )

    def start_loads(c, carry):
        for copy in loads(c):
            copy.start()
        return carry

    lax.fori_loop(0, chunks, start_loads, 0)
    pl.semaphore_wait(barrier, count)

    def start_chunk(c, carry):
        for dd in (-1, 1):

            @pl.when(has[dd][0])
            def _(dd=dd):
                for copy in zcopies(c, dd):
                    copy.start()

        for dr in (-1, 1):

            @pl.when(has[dr][1])
            def _(dr=dr):
                for copy in rcopies(c, dr):
                    copy.start()

        return carry

    for dd, dr in diagonal:

        @pl.when(present(dd, dr))
        def _(dd=dd, dr=dr):
            for copy in ccopies(dd, dr):
                copy.start()

    lax.fori_loop(0, chunks, start_chunk, 0)

    zero = jnp.zeros((SUB, LANES), jnp.float32)

    def pad_q0(z, carry):
        for k in range(4):
            for block in (0, chunks + 1):
                for t in range(tiles + 2):
                    q0[k, z, block, pl.ds(t * SUB, SUB), :] = zero
        return carry

    def pad_q1(z, carry):
        for k in range(4):
            for block in (0, chunks + 1):
                for t in range(tiles + 1):
                    q1[k, z, block, pl.ds(t * SUB, SUB), :] = zero
        return carry

    lax.fori_loop(1, zn + 3, pad_q0, 0)
    lax.fori_loop(0, zn + 2, pad_q1, 0)
    for dd in (-1, 1):
        layer = 1 if dd < 0 else zn + 2

        @pl.when(jnp.logical_not(has[dd][0]))
        def _(layer=layer):
            def clear(c, carry):
                for k in range(4):
                    for t in range(tiles + 2):
                        q0[k, layer, 1 + c, pl.ds(t * SUB, SUB), :] = zero
                return carry

            lax.fori_loop(0, chunks, clear, 0)

    for dr in (-1, 1):
        top = 0 if dr < 0 else SUB + yn

        @pl.when(jnp.logical_not(has[dr][1]))
        def _(top=top):
            def clear(z, carry):
                for k in range(4):
                    for c in range(chunks):
                        q0[k, z, 1 + c, pl.ds(top, SUB), :] = zero
                return carry

            lax.fori_loop(1, zn + 3, clear, 0)

    lane = lax.broadcasted_iota(jnp.int32, (SUB, LANES), 1)
    sublane = lax.broadcasted_iota(jnp.int32, (SUB, LANES), 0)
    first, last = lane == 0, lane == LANES - 1

    for dd, dr in diagonal:

        @pl.when(present(dd, dr))
        def _(dd=dd, dr=dr):
            slot = diagonal.index((dd, dr))
            for copy in ccopies(-dd, -dr):
                copy.wait_recv()
            z = 1 if dd < 0 else zn + 2
            y = SUB - 1 if dr < 0 else SUB + yn
            for c in range(chunks):
                at = pl.ds(c * LANES, LANES)
                q0[0, z, 1 + c, pl.ds(y, 1), :] = corner_d[slot, 0, :, at]
                for k in range(3):
                    q0[1 + k, z, 1 + c, pl.ds(y, 1), :] = corner_v[slot, k, 0, :, at]

    def wait_chunk(c):
        for copy in loads(c):
            copy.wait()
        for dd in (-1, 1):

            @pl.when(has[dd][0])
            def _(dd=dd):
                for copy in zcopies(c, -dd):
                    copy.wait_recv()

        for dr in (-1, 1):

            @pl.when(has[dr][1])
            def _(dr=dr):
                for copy in rcopies(c, -dr):
                    copy.wait_recv()

    low_row = jnp.where(r > 0, -1, 0)
    high_row = jnp.where(r < row_count - 1, yn, yn - 1)
    row_ok = []
    for t in range(tiles + 1):
        y = sublane + (t * SUB - 1)
        row_ok.append((y >= low_row) & (y <= high_row))
    low_z = jnp.where(d > 0, 0, 1)
    high_z = jnp.where(d < depth_count - 1, zn + 1, zn)

    def step_one(c):
        def layer(z, carry):
            inside = (z >= low_z) & (z <= high_z)
            for t in range(tiles + 1):
                new = step_tile(q0, z + 1, 1 + c, SUB - 1 + t * SUB, first, last)
                ok = row_ok[t] & inside
                for k in range(4):
                    q1[k, z, 1 + c, pl.ds(t * SUB, SUB), :] = jnp.where(ok, new[k], 0.0)
            return carry

        lax.fori_loop(0, zn + 2, layer, 0)

    weights = [[0.5 * pal[i, k] for k in range(4)] for i in range(3)]
    thickness = OPTICAL / (zn * depth_count)

    def step_two(c):
        at = cols(c)

        def layer(z, carry):
            out = []
            for t in range(tiles):
                through, *shades = carry[t]
                new = step_tile(q1, z + 1, 1 + c, 1 + t * SUB, first, last)
                rows = pl.ds(t * SUB, SUB)
                out_d[z, rows, at] = new[0]
                for k in range(3):
                    out_v[k, z, rows, at] = new[1 + k]
                beyond = through * jnp.exp((-thickness) * new[0] * new[0])
                emitted = through - beyond
                lit = []
                for i in range(3):
                    dot = weights[i][0] * new[0]
                    for k in range(1, 4):
                        dot = dot + weights[i][k] * new[k]
                    lit.append(shades[i] + emitted * jnp.tanh(dot))
                out.append((beyond, *lit))
            return tuple(out)

        one = jnp.ones((SUB, LANES), jnp.float32)
        start = tuple((one, zero, zero, zero) for _ in range(tiles))
        done = lax.fori_loop(0, zn, layer, start)
        for t in range(tiles):
            through, *shades = done[t]
            rows = pl.ds(t * SUB, SUB)
            for i in range(3):
                piece[c, i, rows, :] = 0.5 * ((1.0 - through) + shades[i])
            piece[c, 3, rows, :] = through

    def pcopy(c, source):
        return pltpu.make_async_remote_copy(
            piece.at[c],
            pieces.at[source],
            psend.at[c],
            precv.at[source],
            device_id={"depth": c, "row": r},
            device_id_type=MESH,
        )

    wait_chunk(0)

    def work(i, carry):
        @pl.when(i + 1 < chunks)
        def _():
            wait_chunk(i + 1)

        @pl.when(i < chunks)
        def _():
            step_one(i)

        @pl.when(i >= 1)
        def _():
            c = i - 1
            step_two(c)

            @pl.when(c != d)
            def _():
                pcopy(c, d).start()

            @pl.when(c == d)
            def _():
                pieces[d] = piece[c]

        return carry

    lax.fori_loop(0, chunks + 1, work, 0)

    def wait_piece(k, carry):
        @pl.when(k != d)
        def _():
            pcopy(k, k).wait_recv()

        return carry

    lax.fori_loop(0, depth_count, wait_piece, 0)

    for t in range(tiles):
        rows = pl.ds(t * SUB, SUB)
        through = pieces[0, 3, rows, :]
        colour = [pieces[0, i, rows, :] for i in range(3)]
        for k in range(1, depth_count):
            for i in range(3):
                colour[i] = colour[i] + through * pieces[k, i, rows, :]
            through = through * pieces[k, 3, rows, :]
        for i in range(3):
            ext[1, i, pl.ds(SUB + t * SUB, SUB), :] = colour[i]
        ext[1, 3, pl.ds(SUB + t * SUB, SUB), :] = 1.0 - through

    def hcopy(dd, dr):
        if dr == 0:
            src = dst = pl.ds(SUB, yn)
        elif dr < 0:
            src, dst = pl.ds(SUB, SUB), pl.ds(SUB + yn, SUB)
        else:
            src, dst = pl.ds(yn, SUB), pl.ds(0, SUB)
        slot = around.index((-dd, -dr))
        return pltpu.make_async_remote_copy(
            ext.at[1, :, src, :],
            ext.at[1 - dd, :, dst, :],
            hsend.at[slot],
            hrecv.at[slot],
            device_id=where_is(dd, dr),
            device_id_type=MESH,
        )

    for dd, dr in around:

        @pl.when(present(dd, dr))
        def _(dd=dd, dr=dr):
            hcopy(dd, dr).start()

    for dd, dr in around:

        @pl.when(present(dd, dr))
        def _(dd=dd, dr=dr):
            hcopy(-dd, -dr).wait_recv()

    for t in range(tiles):
        own = [ext[1, i, pl.ds(SUB + t * SUB, SUB), :] for i in range(4)]
        centre = (own[0] + own[1] + own[2]) * (1.0 / 3.0)
        top = [zero] * 4
        bottom = zero
        for dy in range(-2, 3):
            rows = pl.ds(SUB + t * SUB + dy, SUB)
            y = sublane + (r * yn + t * SUB + dy)
            y_ok = (y >= 0) & (y < yn * row_count)
            mid = [ext[1, i, rows, :] for i in range(4)]
            before = [ext[0, i, rows, :] for i in range(4)]
            after = [ext[2, i, rows, :] for i in range(4)]
            for dx in range(-2, 3):
                x = lane + (d * LANES + dx)
                ok = y_ok & (x >= 0) & (x < LANES * depth_count)
                if dx < 0:
                    pixel = [
                        pltpu.roll(jnp.where(lane >= LANES + dx, before[i], mid[i]), -dx, 1)
                        for i in range(4)
                    ]
                elif dx > 0:
                    pixel = [
                        pltpu.roll(jnp.where(lane < dx, after[i], mid[i]), LANES - dx, 1)
                        for i in range(4)
                    ]
                else:
                    pixel = mid
                pixel = [jnp.where(ok, p, 0.0) for p in pixel]
                space = math.exp(-(dx * dx + dy * dy) / (2.0 * SPACE_SCALE * SPACE_SCALE))
                diff = (pixel[0] + pixel[1] + pixel[2]) * (1.0 / 3.0) - centre
                close = jnp.exp(diff * diff * (-1.0 / (2.0 * RANGE_SCALE * RANGE_SCALE)))
                weight = jnp.where(ok, space * close, 0.0)
                top = [top[i] + weight * pixel[i] for i in range(4)]
                bottom = bottom + weight
        for i in range(4):
            filtered[i, pl.ds(t * SUB, SUB), :] = top[i] / bottom

    def sent(c, carry):
        for dd in (-1, 1):

            @pl.when(has[dd][0])
            def _(dd=dd):
                for copy in zcopies(c, dd):
                    copy.wait_send()

        for dr in (-1, 1):

            @pl.when(has[dr][1])
            def _(dr=dr):
                for copy in rcopies(c, dr):
                    copy.wait_send()

        @pl.when(c != d)
        def _():
            pcopy(c, d).wait_send()

        return carry

    lax.fori_loop(0, chunks, sent, 0)
    for dd, dr in diagonal:

        @pl.when(present(dd, dr))
        def _(dd=dd, dr=dr):
            for copy in ccopies(dd, dr):
                copy.wait_send()

    for dd, dr in around:

        @pl.when(present(dd, dr))
        def _(dd=dd, dr=dr):
            hcopy(dd, dr).wait_send()


def body(depth_count, row_count, density, velocity, palette):
    zn, yn, xn = density.shape
    chunks = xn // LANES
    assert chunks == depth_count and yn % SUB == 0
    f32 = jnp.float32
    dma = pltpu.SemaphoreType.DMA
    vmem = pltpu.VMEM
    return pl.pallas_call(
        functools.partial(kernel, depth_count, row_count),
        out_shape=(
            jax.ShapeDtypeStruct((4, yn, LANES), f32),
            jax.ShapeDtypeStruct(density.shape, f32),
            jax.ShapeDtypeStruct(velocity.shape, f32),
        ),
        in_specs=[
            pl.BlockSpec(memory_space=pl.ANY),
            pl.BlockSpec(memory_space=pl.ANY),
            pl.BlockSpec(memory_space=pltpu.SMEM),
        ],
        out_specs=(pl.BlockSpec(memory_space=vmem),) * 3,
        scratch_shapes=[
            vmem((4, zn + 4, chunks + 2, yn + 2 * SUB, LANES), f32),
            vmem((4, zn + 2, chunks + 2, yn + SUB, LANES), f32),
            vmem((4, 1, 1, xn), f32),
            vmem((4, 3, 1, 1, xn), f32),
            vmem((chunks, 4, yn, LANES), f32),
            vmem((depth_count, 4, yn, LANES), f32),
            vmem((3, 4, yn + 2 * SUB, LANES), f32),
            dma((2, chunks)),
            dma((2, 2, chunks)),
            dma((2, 2, chunks)),
            dma((2, 2, chunks)),
            dma((2, 2, chunks)),
            dma((2, 4)),
            dma((2, 4)),
            dma((chunks,)),
            dma((depth_count,)),
            dma((8,)),
            dma((8,)),
        ],
        compiler_params=pltpu.CompilerParams(
            collective_id=0, has_side_effects=True, vmem_limit_bytes=48 * 2**20
        ),
        name="rheology",
    )(density, velocity, palette)


def solution(mesh):
    in_specs = (P("depth", "row", None), P(None, "depth", "row", None), P())
    out_specs = (P(None, "row", "depth"), P("depth", "row", None), P(None, "depth", "row", None))
    run = functools.partial(body, mesh.shape["depth"], mesh.shape["row"])
    return jax.shard_map(run, mesh=mesh, in_specs=in_specs, out_specs=out_specs, check_vma=False)
```

time: 262 us -> 55.5 us (0.21)
  the two profiles are of different devices: /device:TPU:39 before, /device:TPU:1 now
where the time goes in v1:
time: 55.5 us; the launch traced here: 55.4 us
  Pallas kernels  49.6 us (89%)
  local copies, waits for them, and re-layouts  5.15 us (9%)
  between operations  0.65 us (1%)
    pallas_call x1, Pallas kernels, body(): pl.pallas_call(functools.partial(kernel, depth_count, row_count), out_sha...  49.6 us
    unnamed x7, local copies, waits for them, and re-layouts  5.15 us

profile of v1, /device:TPU:1, one launch (start us, length us, event | category | flops | bytes accessed | tf_op | source)
XLA Modules:
  0.0 55.4 jit_solution(4359311690589740553)
XLA Ops:
  0.6 0.0 copy-start
  0.6 1.2 %copy-done = f32[16,16,1024]{2,1,0:T(8,128)S(1)} copy-done((f32[16,16,1024]{2,1,0:T(8,128)S(1)}, f32[16,16,1024]{2,1,0:T(8,128)}, u32[]{:S(2)}) %copy-start) | copy-done | bytes 1048600
  1.9 0.0 copy-start.1
  1.9 0.7 %copy-done.1 = f32[3,4]{1,0:T(4,128)S(1)} copy-done((f32[3,4]{1,0:T(4,128)S(1)}, f32[3,4]{1,0:T(4,128)}, u32[]{:S(2)}) %copy-start.1) | copy-done | bytes 72
  2.5 49.6 %rheology.1 = (f32[4,16,128]{2,1,0:T(8,128)S(1)}, f32[16,16,1024]{2,1,0:T(8,128)S(1)}, f32[3,16,16,1024]{3,2,1,0:T(8,128)S(1)}) custom-call(f32[16,16,1024]{2,1,0:T(8,128)S(1)} %copy-done, f32[3,16,16,1024]{3,2,1,0:T(8,128)} %vel.1, f32[3,4]{1,0:T(4,128)S(1)} %copy-done.1), custom_call_target="tpu_custom_call" | custom-call | tf_op jit(solution)/shard_map/rheology/pallas_call | solution.py:553
  52.1 0.6 %copy.9 = f32[4,16,128]{2,1,0:T(8,128)} copy(f32[4,16,128]{2,1,0:T(8,128)S(1)} %get-tuple-element.6) | data formatting | bytes 65536
  52.7 1.0 %copy.10 = f32[16,16,1024]{2,1,0:T(8,128)} copy(f32[16,16,1024]{2,1,0:T(8,128)S(1)} %get-tuple-element.7) | data formatting | bytes 2097152
  53.7 1.7 %copy.11 = f32[3,16,16,1024]{3,2,1,0:T(8,128)} copy(f32[3,16,16,1024]{3,2,1,0:T(8,128)S(1)} %get-tuple-element.8) | data formatting | bytes 6291456
Async XLA Ops:
  0.6 1.2 %copy-start = (f32[16,16,1024]{2,1,0:T(8,128)S(1)}, f32[16,16,1024]{2,1,0:T(8,128)}, u32[]{:S(2)}) copy-start(f32[16,16,1024]{2,1,0:T(8,128)} %dens.1) | copy-start | bytes 3145732
  1.9 0.7 %copy-start.1 = (f32[3,4]{1,0:T(4,128)S(1)}, f32[3,4]{1,0:T(4,128)}, u32[]{:S(2)}) copy-start(f32[3,4]{1,0:T(4,128)} %pal.1) | copy-start | bytes 148

commit v2 on v1

--- a/solution.py
+++ b/solution.py
@@ -18,12 +18,17 @@
 MESH = pl.DeviceIdType.MESH
 LANES = 128
 SUB = 8
+PARTS = 2
 
 
 def shifted_pair(before, here, after, first, last):
     left = pltpu.roll(jnp.where(last, before, here), 1, 1)
     right = pltpu.roll(jnp.where(first, after, here), LANES - 1, 1)
     return left, right
+
+
+def divisor(n, most):
+    return max([k for k in range(1, most + 1) if n and n % k == 0], default=1)
 
 
 def step_tile(ref, z, block, row, first, last):
@@ -64,18 +69,22 @@
     row_count,
     dens,
     vel,
-    pal,
-    filtered,
+    pal_hbm,
+    mid,
+    side,
     out_d,
     out_v,
     q0,
     q1,
     corner_d,
     corner_v,
+    middle,
     piece,
     pieces,
-    ext,
+    edge,
+    pal,
     load_sem,
+    pal_sem,
     zsend,
     zrecv,
     rsend,
@@ -217,9 +226,11 @@
         return carry
 
     lax.fori_loop(0, chunks, start_loads, 0)
+    pal_copy = pltpu.make_async_copy(pal_hbm, pal, pal_sem)
+    pal_copy.start()
     pl.semaphore_wait(barrier, count)
 
-    def start_chunk(c, carry):
+    def start_layers(c, carry):
         for dd in (-1, 1):
 
             @pl.when(has[dd][0])
@@ -227,6 +238,9 @@
                 for copy in zcopies(c, dd):
                     copy.start()
 
+        return carry
+
+    def start_rows(c, carry):
         for dr in (-1, 1):
 
             @pl.when(has[dr][1])
@@ -243,7 +257,9 @@
             for copy in ccopies(dd, dr):
                 copy.start()
 
-    lax.fori_loop(0, chunks, start_chunk, 0)
+    start_layers(0, 0)
+    lax.fori_loop(0, chunks, start_rows, 0)
+    lax.fori_loop(1, chunks, start_layers, 0)
 
     zero = jnp.zeros((SUB, LANES), jnp.float32)
 
@@ -292,6 +308,164 @@
     lane = lax.broadcasted_iota(jnp.int32, (SUB, LANES), 1)
     sublane = lax.broadcasted_iota(jnp.int32, (SUB, LANES), 0)
     first, last = lane == 0, lane == LANES - 1
+
+    def wait_layers(c):
+        for dd in (-1, 1):
+
+            @pl.when(has[dd][0])
+            def _(dd=dd):
+                for copy in zcopies(c, -dd):
+                    copy.wait_recv()
+
+    def wait_own(c):
+        for copy in loads(c):
+            copy.wait()
+
+    def wait_rows(c):
+        for dr in (-1, 1):
+
+            @pl.when(has[dr][1])
+            def _(dr=dr):
+                for copy in rcopies(c, -dr):
+                    copy.wait_recv()
+
+    low_row = jnp.where(r > 0, -1, 0)
+    high_row = jnp.where(r < row_count - 1, yn, yn - 1)
+    row_ok = []
+    for t in range(tiles + 1):
+        y = sublane + (t * SUB - 1)
+        row_ok.append((y >= low_row) & (y <= high_row))
+    low_z = jnp.where(d > 0, 0, 1)
+    high_z = jnp.where(d < depth_count - 1, zn + 1, zn)
+
+    def first_step(c, z, which, edge_layer):
+        inside = (z >= low_z) & (z <= high_z) if edge_layer else None
+        for t in which:
+            new = step_tile(q0, z + 1, 1 + c, SUB - 1 + t * SUB, first, last)
+            ok = row_ok[t] if t in (0, tiles) else None
+            if edge_layer:
+                ok = inside if ok is None else ok & inside
+            for k in range(4):
+                q1[k, z, 1 + c, pl.ds(t * SUB, SUB), :] = (
+                    new[k] if ok is None else jnp.where(ok, new[k], 0.0)
+                )
+
+    def first_inner(c, which):
+        def layer(z, carry):
+            first_step(c, z, which, False)
+            return carry
+
+        lax.fori_loop(2, zn, layer, 0, unroll=divisor(zn - 2, 7))
+
+    def first_outer(c):
+        for z in (0, 1, zn, zn + 1):
+            first_step(c, z, range(tiles + 1), z in (0, zn + 1))
+
+    pal_copy.wait()
+    weights = [[0.5 * pal[i, k] for k in range(4)] for i in range(3)]
+    thickness = OPTICAL / (zn * depth_count)
+
+    def second_step(c, z, carry):
+        at = cols(c)
+        out = []
+        for t in range(tiles):
+            through, *shades = carry[t]
+            new = step_tile(q1, z + 1, 1 + c, 1 + t * SUB, first, last)
+            rows = pl.ds(t * SUB, SUB)
+            out_d[z, rows, at] = new[0]
+            for k in range(3):
+                out_v[k, z, rows, at] = new[1 + k]
+            beyond = through * jnp.exp((-thickness) * new[0] * new[0])
+            emitted = through - beyond
+            lit = []
+            for i in range(3):
+                dot = weights[i][0] * new[0]
+                for k in range(1, 4):
+                    dot = dot + weights[i][k] * new[k]
+                lit.append(shades[i] + emitted * jnp.tanh(dot))
+            out.append((beyond, *lit))
+        return tuple(out)
+
+    clear_view = tuple((jnp.ones((SUB, LANES), jnp.float32), zero, zero, zero) for _ in range(tiles))
+
+    def second_inner(c):
+        def layer(z, carry):
+            return second_step(c, z, carry)
+
+        done = lax.fori_loop(2, zn - 2, layer, clear_view, unroll=divisor(zn - 4, 6))
+        for t in range(tiles):
+            for i in range(4):
+                middle[c, i, pl.ds(t * SUB, SUB), :] = done[t][i]
+
+    def second_outer(c):
+        view = clear_view
+        for z in (0, 1):
+            view = second_step(c, z, view)
+        joined = []
+        for t in range(tiles):
+            through, *shades = view[t]
+            own = [middle[c, i, pl.ds(t * SUB, SUB), :] for i in range(4)]
+            joined.append(
+                (through * own[0], *(shades[i] + through * own[1 + i] for i in range(3)))
+            )
+        view = tuple(joined)
+        for z in (zn - 2, zn - 1):
+            view = second_step(c, z, view)
+        for t in range(tiles):
+            through, *shades = view[t]
+            rows = pl.ds(t * SUB, SUB)
+            for i in range(3):
+                piece[c, i, rows, :] = 0.5 * ((1.0 - through) + shades[i])
+            piece[c, 3, rows, :] = through
+
+    def pcopy(c, source):
+        return pltpu.make_async_remote_copy(
+            piece.at[c],
+            pieces.at[source],
+            psend.at[c],
+            precv.at[source],
+            device_id={"depth": c, "row": r},
+            device_id_type=MESH,
+        )
+
+    def hand_over(c):
+        @pl.when(c != d)
+        def _():
+            pcopy(c, d).start()
+
+        @pl.when(c == d)
+        def _():
+            pieces[d] = piece[c]
+
+    wait_own(0)
+
+    def innermost(i, carry):
+        @pl.when(i + 1 < chunks)
+        def _():
+            wait_own(i + 1)
+
+        first_inner(i, range(1, tiles))
+        return carry
+
+    lax.fori_loop(0, chunks, innermost, 0)
+    wait_rows(0)
+
+    def inner(i, carry):
+        @pl.when(i + 1 < chunks)
+        def _():
+            wait_rows(i + 1)
+
+        @pl.when(i < chunks)
+        def _():
+            first_inner(i, (0, tiles))
+
+        @pl.when(i >= 1)
+        def _():
+            second_inner(i - 1)
+
+        return carry
+
+    lax.fori_loop(0, chunks + 1, inner, 0)
 
     for dd, dr in diagonal:
 
@@ -308,117 +482,50 @@
                 for k in range(3):
                     q0[1 + k, z, 1 + c, pl.ds(y, 1), :] = corner_v[slot, k, 0, :, at]
 
-    def wait_chunk(c):
-        for copy in loads(c):
-            copy.wait()
+    wait_layers(0)
+
+    def outer(i, carry):
+        @pl.when(i + 1 < chunks)
+        def _():
+            wait_layers(i + 1)
+
+        @pl.when(i < chunks)
+        def _():
+            first_outer(i)
+
+        @pl.when(i >= 1)
+        def _():
+            second_outer(i - 1)
+            hand_over(i - 1)
+
+        return carry
+
+    lax.fori_loop(0, chunks + 1, outer, 0)
+
+    def sent(c, carry):
         for dd in (-1, 1):
 
             @pl.when(has[dd][0])
             def _(dd=dd):
-                for copy in zcopies(c, -dd):
-                    copy.wait_recv()
+                for copy in zcopies(c, dd):
+                    copy.wait_send()
 
         for dr in (-1, 1):
 
             @pl.when(has[dr][1])
             def _(dr=dr):
-                for copy in rcopies(c, -dr):
-                    copy.wait_recv()
-
-    low_row = jnp.where(r > 0, -1, 0)
-    high_row = jnp.where(r < row_count - 1, yn, yn - 1)
-    row_ok = []
-    for t in range(tiles + 1):
-        y = sublane + (t * SUB - 1)
-        row_ok.append((y >= low_row) & (y <= high_row))
-    low_z = jnp.where(d > 0, 0, 1)
-    high_z = jnp.where(d < depth_count - 1, zn + 1, zn)
-
-    def step_one(c):
-        def layer(z, carry):
-            inside = (z >= low_z) & (z <= high_z)
-            for t in range(tiles + 1):
-                new = step_tile(q0, z + 1, 1 + c, SUB - 1 + t * SUB, first, last)
-                ok = row_ok[t] & inside
-                for k in range(4):
-                    q1[k, z, 1 + c, pl.ds(t * SUB, SUB), :] = jnp.where(ok, new[k], 0.0)
-            return carry
-
-        lax.fori_loop(0, zn + 2, layer, 0)
-
-    weights = [[0.5 * pal[i, k] for k in range(4)] for i in range(3)]
-    thickness = OPTICAL / (zn * depth_count)
-
-    def step_two(c):
-        at = cols(c)
-
-        def layer(z, carry):
-            out = []
-            for t in range(tiles):
-                through, *shades = carry[t]
-                new = step_tile(q1, z + 1, 1 + c, 1 + t * SUB, first, last)
-                rows = pl.ds(t * SUB, SUB)
-                out_d[z, rows, at] = new[0]
-                for k in range(3):
-                    out_v[k, z, rows, at] = new[1 + k]
-                beyond = through * jnp.exp((-thickness) * new[0] * new[0])
-                emitted = through - beyond
-                lit = []
-                for i in range(3):
-                    dot = weights[i][0] * new[0]
-                    for k in range(1, 4):
-                        dot = dot + weights[i][k] * new[k]
-                    lit.append(shades[i] + emitted * jnp.tanh(dot))
-                out.append((beyond, *lit))
-            return tuple(out)
-
-        one = jnp.ones((SUB, LANES), jnp.float32)
-        start = tuple((one, zero, zero, zero) for _ in range(tiles))
-        done = lax.fori_loop(0, zn, layer, start)
-        for t in range(tiles):
-            through, *shades = done[t]
-            rows = pl.ds(t * SUB, SUB)
-            for i in range(3):
-                piece[c, i, rows, :] = 0.5 * ((1.0 - through) + shades[i])
-            piece[c, 3, rows, :] = through
-
-    def pcopy(c, source):
-        return pltpu.make_async_remote_copy(
-            piece.at[c],
-            pieces.at[source],
-            psend.at[c],
-            precv.at[source],
-            device_id={"depth": c, "row": r},
-            device_id_type=MESH,
-        )
-
-    wait_chunk(0)
-
-    def work(i, carry):
-        @pl.when(i + 1 < chunks)
-        def _():
-            wait_chunk(i + 1)
-
-        @pl.when(i < chunks)
-        def _():
-            step_one(i)
-
-        @pl.when(i >= 1)
-        def _():
-            c = i - 1
-            step_two(c)
-
-            @pl.when(c != d)
-            def _():
-                pcopy(c, d).start()
-
-            @pl.when(c == d)
-            def _():
-                pieces[d] = piece[c]
-
-        return carry
-
-    lax.fori_loop(0, chunks + 1, work, 0)
+                for copy in rcopies(c, dr):
+                    copy.wait_send()
+
+        return carry
+
+    lax.fori_loop(0, chunks, sent, 0)
+    for dd, dr in diagonal:
+
+        @pl.when(present(dd, dr))
+        def _(dd=dd, dr=dr):
+            for copy in ccopies(dd, dr):
+                copy.wait_send()
 
     def wait_piece(k, carry):
         @pl.when(k != d)
@@ -437,21 +544,31 @@
             for i in range(3):
                 colour[i] = colour[i] + through * pieces[k, i, rows, :]
             through = through * pieces[k, 3, rows, :]
-        for i in range(3):
-            ext[1, i, pl.ds(SUB + t * SUB, SUB), :] = colour[i]
-        ext[1, 3, pl.ds(SUB + t * SUB, SUB), :] = 1.0 - through
+        pixel = colour + [1.0 - through]
+        rows = pl.ds(SUB + t * SUB, SUB)
+        left, right = pixel[0], pltpu.roll(pixel[0], 2, 1)
+        for i in range(4):
+            mid[i, rows, :] = pixel[i]
+            if i:
+                left = jnp.where(lane >= 2 * i, pltpu.roll(pixel[i], 2 * i, 1), left)
+                right = jnp.where(lane >= 2 * i, pltpu.roll(pixel[i], 2 * i + 2, 1), right)
+        edge[0, rows, :] = left
+        edge[1, rows, :] = right
 
     def hcopy(dd, dr):
         if dr == 0:
             src = dst = pl.ds(SUB, yn)
         elif dr < 0:
-            src, dst = pl.ds(SUB, SUB), pl.ds(SUB + yn, SUB)
+            src, dst = pl.ds(SUB, 2), pl.ds(SUB + yn, 2)
         else:
-            src, dst = pl.ds(yn, SUB), pl.ds(0, SUB)
+            src, dst = pl.ds(SUB + yn - 2, 2), pl.ds(SUB - 2, 2)
         slot = around.index((-dd, -dr))
+        if dd:
+            ends = edge.at[(dd + 1) // 2, src, :], side.at[(1 - dd) // 2, dst, :]
+        else:
+            ends = mid.at[:, src, :], mid.at[:, dst, :]
         return pltpu.make_async_remote_copy(
-            ext.at[1, :, src, :],
-            ext.at[1 - dd, :, dst, :],
+            *ends,
             hsend.at[slot],
             hrecv.at[slot],
             device_id=where_is(dd, dr),
@@ -464,14 +581,49 @@
         def _(dd=dd, dr=dr):
             hcopy(dd, dr).start()
 
+    def piece_sent(c, carry):
+        @pl.when(c != d)
+        def _():
+            pcopy(c, d).wait_send()
+
+        return carry
+
+    lax.fori_loop(0, chunks, piece_sent, 0)
     for dd, dr in around:
 
         @pl.when(present(dd, dr))
         def _(dd=dd, dr=dr):
             hcopy(-dd, -dr).wait_recv()
 
+    for dd, dr in around:
+
+        @pl.when(present(dd, dr))
+        def _(dd=dd, dr=dr):
+            hcopy(dd, dr).wait_send()
+
+
+def finish(depth_count, row_count, picture, side, settled_d, settled_v, filtered, out_d, out_v, sem):
+    zn = settled_d.shape[0]
+    part = zn // PARTS
+    copies = []
+    for p in range(PARTS):
+        z = pl.ds(p * part, part)
+        copies.append(pltpu.make_async_copy(settled_d.at[z], out_d.at[z], sem.at[0, p]))
+        for k in range(3):
+            copies.append(
+                pltpu.make_async_copy(settled_v.at[k, z], out_v.at[k, z], sem.at[1 + k, p])
+            )
+    for copy in copies:
+        copy.start()
+    yn = filtered.shape[1]
+    tiles = yn // SUB
+    d = lax.axis_index("depth")
+    r = lax.axis_index("row")
+    lane = lax.broadcasted_iota(jnp.int32, (SUB, LANES), 1)
+    sublane = lax.broadcasted_iota(jnp.int32, (SUB, LANES), 0)
+    zero = jnp.zeros((SUB, LANES), jnp.float32)
     for t in range(tiles):
-        own = [ext[1, i, pl.ds(SUB + t * SUB, SUB), :] for i in range(4)]
+        own = [picture[i, pl.ds(SUB + t * SUB, SUB), :] for i in range(4)]
         centre = (own[0] + own[1] + own[2]) * (1.0 / 3.0)
         top = [zero] * 4
         bottom = zero
@@ -479,9 +631,9 @@
             rows = pl.ds(SUB + t * SUB + dy, SUB)
             y = sublane + (r * yn + t * SUB + dy)
             y_ok = (y >= 0) & (y < yn * row_count)
-            mid = [ext[1, i, rows, :] for i in range(4)]
-            before = [ext[0, i, rows, :] for i in range(4)]
-            after = [ext[2, i, rows, :] for i in range(4)]
+            mid = [picture[i, rows, :] for i in range(4)]
+            before = [pltpu.roll(side[0, rows, :], LANES - 2 - 2 * i, 1) for i in range(4)]
+            after = [pltpu.roll(side[1, rows, :], (LANES - 2 * i) % LANES, 1) for i in range(4)]
             for dx in range(-2, 3):
                 x = lane + (d * LANES + dx)
                 ok = y_ok & (x >= 0) & (x < LANES * depth_count)
@@ -506,41 +658,8 @@
                 bottom = bottom + weight
         for i in range(4):
             filtered[i, pl.ds(t * SUB, SUB), :] = top[i] / bottom
-
-    def sent(c, carry):
-        for dd in (-1, 1):
-
-            @pl.when(has[dd][0])
-            def _(dd=dd):
-                for copy in zcopies(c, dd):
-                    copy.wait_send()
-
-        for dr in (-1, 1):
-
-            @pl.when(has[dr][1])
-            def _(dr=dr):
-                for copy in rcopies(c, dr):
-                    copy.wait_send()
-
-        @pl.when(c != d)
-        def _():
-            pcopy(c, d).wait_send()
-
-        return carry
-
-    lax.fori_loop(0, chunks, sent, 0)
-    for dd, dr in diagonal:
-
-        @pl.when(present(dd, dr))
-        def _(dd=dd, dr=dr):
-            for copy in ccopies(dd, dr):
-                copy.wait_send()
-
-    for dd, dr in around:
-
-        @pl.when(present(dd, dr))
-        def _(dd=dd, dr=dr):
-            hcopy(dd, dr).wait_send()
+    for copy in copies:
+        copy.wait()
 
 
 def body(depth_count, row_count, density, velocity, palette):
@@ -550,28 +669,30 @@
     f32 = jnp.float32
     dma = pltpu.SemaphoreType.DMA
     vmem = pltpu.VMEM
-    return pl.pallas_call(
+    hbm = pl.BlockSpec(memory_space=pltpu.HBM)
+    on_chip = pl.BlockSpec(memory_space=vmem)
+    picture, side, settled_d, settled_v = pl.pallas_call(
         functools.partial(kernel, depth_count, row_count),
         out_shape=(
-            jax.ShapeDtypeStruct((4, yn, LANES), f32),
+            jax.ShapeDtypeStruct((4, yn + 2 * SUB, LANES), f32),
+            jax.ShapeDtypeStruct((2, yn + 2 * SUB, LANES), f32),
             jax.ShapeDtypeStruct(density.shape, f32),
             jax.ShapeDtypeStruct(velocity.shape, f32),
         ),
-        in_specs=[
-            pl.BlockSpec(memory_space=pl.ANY),
-            pl.BlockSpec(memory_space=pl.ANY),
-            pl.BlockSpec(memory_space=pltpu.SMEM),
-        ],
-        out_specs=(pl.BlockSpec(memory_space=vmem),) * 3,
+        in_specs=[hbm, hbm, hbm],
+        out_specs=(on_chip,) * 4,
         scratch_shapes=[
             vmem((4, zn + 4, chunks + 2, yn + 2 * SUB, LANES), f32),
             vmem((4, zn + 2, chunks + 2, yn + SUB, LANES), f32),
             vmem((4, 1, 1, xn), f32),
             vmem((4, 3, 1, 1, xn), f32),
             vmem((chunks, 4, yn, LANES), f32),
+            vmem((chunks, 4, yn, LANES), f32),
             vmem((depth_count, 4, yn, LANES), f32),
-            vmem((3, 4, yn + 2 * SUB, LANES), f32),
+            vmem((2, yn + 2 * SUB, LANES), f32),
+            pltpu.SMEM((3, 4), f32),
             dma((2, chunks)),
+            dma,
             dma((2, 2, chunks)),
             dma((2, 2, chunks)),
             dma((2, 2, chunks)),
@@ -587,7 +708,20 @@
             collective_id=0, has_side_effects=True, vmem_limit_bytes=48 * 2**20
         ),
         name="rheology",
-    )(density, velocity, palette)
+    )(*(pltpu.with_memory_space_constraint(v, pltpu.HBM) for v in (density, velocity, palette)))
+    return pl.pallas_call(
+        functools.partial(finish, depth_count, row_count),
+        out_shape=(
+            jax.ShapeDtypeStruct((4, yn, LANES), f32),
+            jax.ShapeDtypeStruct(density.shape, f32),
+            jax.ShapeDtypeStruct(velocity.shape, f32),
+        ),
+        in_specs=[on_chip] * 4,
+        out_specs=(on_chip, hbm, hbm),
+        scratch_shapes=[dma((4, PARTS))],
+        compiler_params=pltpu.CompilerParams(vmem_limit_bytes=8 * 2**20),
+        name="finish",
+    )(picture, side, settled_d, settled_v)
 
 
 def solution(mesh):

time: 55.5 us -> 37.1 us (0.67)
  the two profiles are of different devices: /device:TPU:1 before, /device:TPU:103 now
where the time goes in v2:
time: 37.1 us; the launch traced here: 37 us
  Pallas kernels  36.4 us (98%)
  between operations  0.64 us (2%)
    pallas_call x1, Pallas kernels, body(): pl.pallas_call(functools.partial(kernel, depth_count, row_count), out_sha...  33.2 us
    pallas_call x1, Pallas kernels, body(): pl.pallas_call(functools.partial(finish, depth_count, row_count), out_sha...  3.17 us

profile of v2, /device:TPU:103, one launch (start us, length us, event | category | flops | bytes accessed | tf_op | source)
XLA Modules:
  0.0 37.0 jit_solution(15166275444185260519)
XLA Ops:
  0.6 33.2 %rheology.1 = (f32[4,32,128]{2,1,0:T(8,128)S(1)}, f32[2,32,128]{2,1,0:T(8,128)S(1)}, f32[16,16,1024]{2,1,0:T(8,128)S(1)}, f32[3,16,16,1024]{3,2,1,0:T(8,128)S(1)}) custom-call(f32[16,16,1024]{2,1,0:T(8,128)} %dens.1, f32[3,16,16,1024]{3,2,1,0:T(8,128)} %vel.1, f32[3,4]{1,0:T(4,128)} %pal_hbm.1), custom_call_target="tpu_custom_call" | custom-call | tf_op jit(solution)/shard_map/rheology/pallas_call | solution.py:674
  33.8 3.2 %finish.1 = (f32[4,16,128]{2,1,0:T(8,128)}, f32[16,16,1024]{2,1,0:T(8,128)}, f32[3,16,16,1024]{3,2,1,0:T(8,128)}) custom-call(f32[4,32,128]{2,1,0:T(8,128)S(1)} %get-tuple-element.7.picture, f32[2,32,128]{2,1,0:T(8,128)S(1)} %get-tuple-element.8.side, f32[16,16,1024]{2,1,0:T(8,128)S(1)} %get-tuple-element.9.settled_d, ...), custom_call_target="tpu_custom_call" | custom-call | tf_op jit(solution)/shard_map/finish/pallas_call | solution.py:712

commit v3 on v2

--- a/solution.py
+++ b/solution.py
@@ -19,6 +19,7 @@
 LANES = 128
 SUB = 8
 PARTS = 2
+FAR = 1.0e6
 
 
 def shifted_pair(before, here, after, first, last):
@@ -78,7 +79,6 @@
     q1,
     corner_d,
     corner_v,
-    middle,
     piece,
     pieces,
     edge,
@@ -91,6 +91,7 @@
     rrecv,
     csend,
     crecv,
+    word,
     psend,
     precv,
     hsend,
@@ -113,26 +114,30 @@
     def where_is(dd, dr):
         return {"depth": d + dd, "row": r + dr}
 
-    around = [(dd, dr) for dd in (-1, 0, 1) for dr in (-1, 0, 1) if dd or dr]
     diagonal = [(dd, dr) for dd in (-1, 1) for dr in (-1, 1)]
-
+    around = diagonal + [(-1, 0), (1, 0), (0, -1), (0, 1)]
+
+    ring = [{"depth": lax.rem(d + k, depth_count), "row": r} for k in (1, depth_count - 1)]
     barrier = pltpu.get_barrier_semaphore()
-    count = jnp.int32(depth_count - 1)
-    for dd, dr in around:
-        if dr == 0:
-            continue
-        ok = present(dd, dr)
+    count = jnp.int32(2)
+    for place in ring:
+        pl.semaphore_signal(barrier, inc=1, device_id=place, device_id_type=MESH)
+    for dr in (-1, 1):
+        ok = has[dr][1]
         count = count + ok.astype(jnp.int32)
 
         @pl.when(ok)
-        def _(dd=dd, dr=dr):
-            pl.semaphore_signal(barrier, inc=1, device_id=where_is(dd, dr), device_id_type=MESH)
-
-    for k in range(1, depth_count):
-        other = lax.rem(d + k, depth_count)
-        pl.semaphore_signal(
-            barrier, inc=1, device_id={"depth": other, "row": r}, device_id_type=MESH
-        )
+        def _(dr=dr):
+            pl.semaphore_signal(barrier, inc=1, device_id=where_is(0, dr), device_id_type=MESH)
+
+    words = depth_count // 2 - 1
+
+    def pass_word(k):
+        for place in ring:
+            pl.semaphore_signal(word.at[k], inc=1, device_id=place, device_id_type=MESH)
+
+    def hear_word(k):
+        pl.semaphore_wait(word.at[k], 2)
 
     def cols(c):
         return pl.ds(pl.multiple_of(c * LANES, LANES), LANES)
@@ -250,17 +255,10 @@
 
         return carry
 
-    for dd, dr in diagonal:
-
-        @pl.when(present(dd, dr))
-        def _(dd=dd, dr=dr):
-            for copy in ccopies(dd, dr):
-                copy.start()
-
     start_layers(0, 0)
+    pass_word(0)
+    start_layers(1, 0)
     lax.fori_loop(0, chunks, start_rows, 0)
-    lax.fori_loop(1, chunks, start_layers, 0)
-
     zero = jnp.zeros((SUB, LANES), jnp.float32)
 
     def pad_q0(z, carry):
@@ -304,6 +302,18 @@
                 return carry
 
             lax.fori_loop(1, zn + 3, clear, 0)
+
+    hear_word(0)
+    if words > 1:
+        pass_word(1)
+    for dd, dr in diagonal:
+
+        @pl.when(present(dd, dr))
+        def _(dd=dd, dr=dr):
+            for copy in ccopies(dd, dr):
+                copy.start()
+
+    lax.fori_loop(2, chunks, start_layers, 0)
 
     lane = lax.broadcasted_iota(jnp.int32, (SUB, LANES), 1)
     sublane = lax.broadcasted_iota(jnp.int32, (SUB, LANES), 0)
@@ -388,31 +398,13 @@
 
     clear_view = tuple((jnp.ones((SUB, LANES), jnp.float32), zero, zero, zero) for _ in range(tiles))
 
-    def second_inner(c):
+    def second(c):
         def layer(z, carry):
             return second_step(c, z, carry)
 
-        done = lax.fori_loop(2, zn - 2, layer, clear_view, unroll=divisor(zn - 4, 6))
+        done = lax.fori_loop(0, zn, layer, clear_view, unroll=divisor(zn, 8))
         for t in range(tiles):
-            for i in range(4):
-                middle[c, i, pl.ds(t * SUB, SUB), :] = done[t][i]
-
-    def second_outer(c):
-        view = clear_view
-        for z in (0, 1):
-            view = second_step(c, z, view)
-        joined = []
-        for t in range(tiles):
-            through, *shades = view[t]
-            own = [middle[c, i, pl.ds(t * SUB, SUB), :] for i in range(4)]
-            joined.append(
-                (through * own[0], *(shades[i] + through * own[1 + i] for i in range(3)))
-            )
-        view = tuple(joined)
-        for z in (zn - 2, zn - 1):
-            view = second_step(c, z, view)
-        for t in range(tiles):
-            through, *shades = view[t]
+            through, *shades = done[t]
             rows = pl.ds(t * SUB, SUB)
             for i in range(3):
                 piece[c, i, rows, :] = 0.5 * ((1.0 - through) + shades[i])
@@ -448,24 +440,10 @@
         return carry
 
     lax.fori_loop(0, chunks, innermost, 0)
-    wait_rows(0)
-
-    def inner(i, carry):
-        @pl.when(i + 1 < chunks)
-        def _():
-            wait_rows(i + 1)
-
-        @pl.when(i < chunks)
-        def _():
-            first_inner(i, (0, tiles))
-
-        @pl.when(i >= 1)
-        def _():
-            second_inner(i - 1)
-
-        return carry
-
-    lax.fori_loop(0, chunks + 1, inner, 0)
+    if words > 1:
+        hear_word(1)
+    if words > 2:
+        pass_word(2)
 
     for dd, dr in diagonal:
 
@@ -482,25 +460,41 @@
                 for k in range(3):
                     q0[1 + k, z, 1 + c, pl.ds(y, 1), :] = corner_v[slot, k, 0, :, at]
 
+    wait_rows(0)
     wait_layers(0)
 
-    def outer(i, carry):
+    def work(i, carry):
         @pl.when(i + 1 < chunks)
         def _():
+            wait_rows(i + 1)
             wait_layers(i + 1)
 
+        @pl.when(i == chunks - 2)
+        def _():
+            for c in range(2, chunks - 3):
+                hand_over(c)
+
         @pl.when(i < chunks)
         def _():
+            first_inner(i, (0, tiles))
             first_outer(i)
 
+        for k in range(2, words):
+
+            @pl.when(i == k - 1)
+            def _(k=k):
+                hear_word(k)
+                if k + 1 < words:
+                    pass_word(k + 1)
+
         @pl.when(i >= 1)
         def _():
-            second_outer(i - 1)
-            hand_over(i - 1)
-
-        return carry
-
-    lax.fori_loop(0, chunks + 1, outer, 0)
+            second(i - 1)
+            pl.when((i <= 2) | (i >= chunks - 2))(lambda: hand_over(i - 1))
+
+        return carry
+
+    lax.fori_loop(0, chunks + 1, work, 0)
 
     def sent(c, carry):
         for dd in (-1, 1):
@@ -602,7 +596,7 @@
             hcopy(dd, dr).wait_send()
 
 
-def finish(depth_count, row_count, picture, side, settled_d, settled_v, filtered, out_d, out_v, sem):
+def finish(depth_count, row_count, picture, side, settled_d, settled_v, filtered, out_d, out_v, moved, sem):
     zn = settled_d.shape[0]
     part = zn // PARTS
     copies = []
@@ -622,42 +616,58 @@
     lane = lax.broadcasted_iota(jnp.int32, (SUB, LANES), 1)
     sublane = lax.broadcasted_iota(jnp.int32, (SUB, LANES), 0)
     zero = jnp.zeros((SUB, LANES), jnp.float32)
+    for t in range(tiles + 2):
+        rows = pl.ds(t * SUB, SUB)
+        y = sublane + (r * yn + (t - 1) * SUB)
+        y_ok = (y >= 0) & (y < yn * row_count)
+        own = [picture[i, rows, :] for i in range(4)]
+        low, high = side[0, rows, :], side[1, rows, :]
+        before = [
+            jnp.where(lane >= LANES - 2, pltpu.roll(low, LANES - 2 - 2 * i, 1), own[i])
+            for i in range(4)
+        ]
+        after = [
+            jnp.where(lane < 2, pltpu.roll(high, LANES - 2 * i, 1) if i else high, own[i])
+            for i in range(4)
+        ]
+        for dx in range(-2, 3):
+            x = lane + (d * LANES + dx)
+            ok = y_ok & (x >= 0) & (x < LANES * depth_count)
+            if dx < 0:
+                pixel = [
+                    pltpu.roll(jnp.where(lane >= LANES + dx, before[i], own[i]), -dx, 1)
+                    for i in range(4)
+                ]
+            elif dx > 0:
+                pixel = [
+                    pltpu.roll(jnp.where(lane < dx, after[i], own[i]), LANES - dx, 1)
+                    for i in range(4)
+                ]
+            else:
+                pixel = own
+            pixel = [jnp.where(ok, p, 0.0) for p in pixel]
+            for i in range(4):
+                moved[dx + 2, i, rows, :] = pixel[i]
+            moved[dx + 2, 4, rows, :] = jnp.where(
+                ok, (pixel[0] + pixel[1] + pixel[2]) * (1.0 / 3.0), FAR
+            )
     for t in range(tiles):
-        own = [picture[i, pl.ds(SUB + t * SUB, SUB), :] for i in range(4)]
-        centre = (own[0] + own[1] + own[2]) * (1.0 / 3.0)
+        centre = moved[2, 4, pl.ds(SUB + t * SUB, SUB), :]
         top = [zero] * 4
         bottom = zero
         for dy in range(-2, 3):
             rows = pl.ds(SUB + t * SUB + dy, SUB)
-            y = sublane + (r * yn + t * SUB + dy)
-            y_ok = (y >= 0) & (y < yn * row_count)
-            mid = [picture[i, rows, :] for i in range(4)]
-            before = [pltpu.roll(side[0, rows, :], LANES - 2 - 2 * i, 1) for i in range(4)]
-            after = [pltpu.roll(side[1, rows, :], (LANES - 2 * i) % LANES, 1) for i in range(4)]
             for dx in range(-2, 3):
-                x = lane + (d * LANES + dx)
-                ok = y_ok & (x >= 0) & (x < LANES * depth_count)
-                if dx < 0:
-                    pixel = [
-                        pltpu.roll(jnp.where(lane >= LANES + dx, before[i], mid[i]), -dx, 1)
-                        for i in range(4)
-                    ]
-                elif dx > 0:
-                    pixel = [
-                        pltpu.roll(jnp.where(lane < dx, after[i], mid[i]), LANES - dx, 1)
-                        for i in range(4)
-                    ]
-                else:
-                    pixel = mid
-                pixel = [jnp.where(ok, p, 0.0) for p in pixel]
                 space = math.exp(-(dx * dx + dy * dy) / (2.0 * SPACE_SCALE * SPACE_SCALE))
-                diff = (pixel[0] + pixel[1] + pixel[2]) * (1.0 / 3.0) - centre
+                diff = moved[dx + 2, 4, rows, :] - centre
                 close = jnp.exp(diff * diff * (-1.0 / (2.0 * RANGE_SCALE * RANGE_SCALE)))
-                weight = jnp.where(ok, space * close, 0.0)
-                top = [top[i] + weight * pixel[i] for i in range(4)]
+                weight = space * close
+                top = [top[i] + weight * moved[dx + 2, i, rows, :] for i in range(4)]
                 bottom = bottom + weight
+        inverse = 1.0 / bottom
         for i in range(4):
-            filtered[i, pl.ds(t * SUB, SUB), :] = top[i] / bottom
+            filtered[i, pl.ds(t * SUB, SUB), :] = top[i] * inverse
+
     for copy in copies:
         copy.wait()
 
@@ -687,7 +697,6 @@
             vmem((4, 1, 1, xn), f32),
             vmem((4, 3, 1, 1, xn), f32),
             vmem((chunks, 4, yn, LANES), f32),
-            vmem((chunks, 4, yn, LANES), f32),
             vmem((depth_count, 4, yn, LANES), f32),
             vmem((2, yn + 2 * SUB, LANES), f32),
             pltpu.SMEM((3, 4), f32),
@@ -699,6 +708,7 @@
             dma((2, 2, chunks)),
             dma((2, 4)),
             dma((2, 4)),
+            pltpu.SemaphoreType.REGULAR((max(1, depth_count // 2 - 1),)),
             dma((chunks,)),
             dma((depth_count,)),
             dma((8,)),
@@ -718,7 +728,7 @@
         ),
         in_specs=[on_chip] * 4,
         out_specs=(on_chip, hbm, hbm),
-        scratch_shapes=[dma((4, PARTS))],
+        scratch_shapes=[vmem((5, 5, yn + 2 * SUB, LANES), f32), dma((4, PARTS))],
         compiler_params=pltpu.CompilerParams(vmem_limit_bytes=8 * 2**20),
         name="finish",
     )(picture, side, settled_d, settled_v)

time: 37.1 us -> 35.1 us (0.946)
  the two profiles are of different devices: /device:TPU:103 before, /device:TPU:1 now
where the time goes in v3:
time: 35.1 us; the launch traced here: 35 us
  Pallas kernels  34.4 us (98%)
  between operations  0.64 us (2%)
    pallas_call x1, Pallas kernels, body(): pl.pallas_call(functools.partial(kernel, depth_count, row_count), out_sha...  31.6 us
    pallas_call x1, Pallas kernels, body(): pl.pallas_call(functools.partial(finish, depth_count, row_count), out_sha...  2.82 us

profile of v3, /device:TPU:1, one launch (start us, length us, event | category | flops | bytes accessed | tf_op | source)
XLA Modules:
  0.0 35.0 jit_solution(8215934100584739785)
XLA Ops:
  0.6 31.6 %rheology.1 = (f32[4,32,128]{2,1,0:T(8,128)S(1)}, f32[2,32,128]{2,1,0:T(8,128)S(1)}, f32[16,16,1024]{2,1,0:T(8,128)S(1)}, f32[3,16,16,1024]{3,2,1,0:T(8,128)S(1)}) custom-call(f32[16,16,1024]{2,1,0:T(8,128)} %dens.1, f32[3,16,16,1024]{3,2,1,0:T(8,128)} %vel.1, f32[3,4]{1,0:T(4,128)} %pal_hbm.1), custom_call_target="tpu_custom_call" | custom-call | tf_op jit(solution)/shard_map/rheology/pallas_call | solution.py:684
  32.2 2.8 %finish.1 = (f32[4,16,128]{2,1,0:T(8,128)}, f32[16,16,1024]{2,1,0:T(8,128)}, f32[3,16,16,1024]{3,2,1,0:T(8,128)}) custom-call(f32[4,32,128]{2,1,0:T(8,128)S(1)} %get-tuple-element.7.picture, f32[2,32,128]{2,1,0:T(8,128)S(1)} %get-tuple-element.8.side, f32[16,16,1024]{2,1,0:T(8,128)S(1)} %get-tuple-element.9.settled_d, ...), custom_call_target="tpu_custom_call" | custom-call | tf_op jit(solution)/shard_map/finish/pallas_call | solution.py:722

commit v4 on v3

--- a/solution.py
+++ b/solution.py
@@ -18,7 +18,7 @@
 MESH = pl.DeviceIdType.MESH
 LANES = 128
 SUB = 8
-PARTS = 2
+PARTS = 1
 FAR = 1.0e6
 
 
@@ -467,6 +467,13 @@
         @pl.when(i + 1 < chunks)
         def _():
             wait_rows(i + 1)
+
+        @pl.when(i < chunks)
+        def _():
+            first_inner(i, (0, tiles))
+
+        @pl.when(i + 1 < chunks)
+        def _():
             wait_layers(i + 1)
 
         @pl.when(i == chunks - 2)
@@ -476,7 +483,6 @@
 
         @pl.when(i < chunks)
         def _():
-            first_inner(i, (0, tiles))
             first_outer(i)
 
         for k in range(2, words):
@@ -521,23 +527,22 @@
             for copy in ccopies(dd, dr):
                 copy.wait_send()
 
-    def wait_piece(k, carry):
+    seen = []
+    for k in range(depth_count):
+
         @pl.when(k != d)
-        def _():
+        def _(k=k):
             pcopy(k, k).wait_recv()
 
-        return carry
-
-    lax.fori_loop(0, depth_count, wait_piece, 0)
-
+        for t in range(tiles):
+            own = [pieces[k, i, pl.ds(t * SUB, SUB), :] for i in range(4)]
+            if k == 0:
+                seen.append(own)
+            else:
+                through = seen[t][3]
+                seen[t] = [seen[t][i] + through * own[i] for i in range(3)] + [through * own[3]]
     for t in range(tiles):
-        rows = pl.ds(t * SUB, SUB)
-        through = pieces[0, 3, rows, :]
-        colour = [pieces[0, i, rows, :] for i in range(3)]
-        for k in range(1, depth_count):
-            for i in range(3):
-                colour[i] = colour[i] + through * pieces[k, i, rows, :]
-            through = through * pieces[k, 3, rows, :]
+        *colour, through = seen[t]
         pixel = colour + [1.0 - through]
         rows = pl.ds(SUB + t * SUB, SUB)
         left, right = pixel[0], pltpu.roll(pixel[0], 2, 1)

time: 35.1 us -> 35 us (level)
  Pallas kernels: 34.4 us -> 34 us
    pallas_call x1, Pallas kernels: 31.6 us -> 31.2 us  [body(): pl.pallas_call(functools.partial(kernel, depth_count, row_count), out_sha...]
where the time goes in v4:
time: 35 us; the launch traced here: 34.6 us
  Pallas kernels  34 us (97%)
  between operations  0.64 us (2%)
    pallas_call x1, Pallas kernels, body(): pl.pallas_call(functools.partial(kernel, depth_count, row_count), out_sha...  31.2 us
    pallas_call x1, Pallas kernels, body(): pl.pallas_call(functools.partial(finish, depth_count, row_count), out_sha...  2.79 us

profile of v4, /device:TPU:1, one launch (start us, length us, event | category | flops | bytes accessed | tf_op | source)
XLA Modules:
  0.0 34.6 jit_solution(17786921417488240613)
XLA Ops:
  0.6 31.2 %rheology.1 = (f32[4,32,128]{2,1,0:T(8,128)S(1)}, f32[2,32,128]{2,1,0:T(8,128)S(1)}, f32[16,16,1024]{2,1,0:T(8,128)S(1)}, f32[3,16,16,1024]{3,2,1,0:T(8,128)S(1)}) custom-call(f32[16,16,1024]{2,1,0:T(8,128)} %dens.1, f32[3,16,16,1024]{3,2,1,0:T(8,128)} %vel.1, f32[3,4]{1,0:T(4,128)} %pal_hbm.1), custom_call_target="tpu_custom_call" | custom-call | tf_op jit(solution)/shard_map/rheology/pallas_call | solution.py:689
  31.8 2.8 %finish.1 = (f32[4,16,128]{2,1,0:T(8,128)}, f32[16,16,1024]{2,1,0:T(8,128)}, f32[3,16,16,1024]{3,2,1,0:T(8,128)}) custom-call(f32[4,32,128]{2,1,0:T(8,128)S(1)} %get-tuple-element.7.picture, f32[2,32,128]{2,1,0:T(8,128)S(1)} %get-tuple-element.8.side, f32[16,16,1024]{2,1,0:T(8,128)S(1)} %get-tuple-element.9.settled_d, ...), custom_call_target="tpu_custom_call" | custom-call | tf_op jit(solution)/shard_map/finish/pallas_call | solution.py:727
